TPU v7x, 32 devices: a whole 2x2x4 slice. The times are simulated.
32 devices in a mesh: groups: 2 (over y), expert: 16 (over z, x, core).
Axes of the slice: x: 2, y: 2, z: 4, core: 2. Of those that a mesh axis runs over, the one named last changes fastest.
Arguments:
- queries: bfloat16 [192, 6144], P(('groups', 'expert')), parts along dimension 0, may hold values from -8 to 8
- tree_key_value: bfloat16 [192, 2, 1024], P(('groups', 'expert')), parts along dimension 0, may hold values from -6 to 6
- key_value_cache: bfloat16 [32, 2, 512, 1024], P(('groups', 'expert')), parts along dimension 0, may hold values from -8 to 8
- lengths: int32 [32], P(('groups', 'expert')), parts along dimension 0, may hold values from 128 to 512, as said below
- parents: int32 [192], P(('groups', 'expert')), parts along dimension 0, may hold values from 0 to 4, as said below
- residual: bfloat16 [192, 6144], P(('groups', 'expert')), parts along dimension 0, may hold values from -6 to 6
- ffn_gain: bfloat16 [6144], replicated, may hold values from 0.099609375 to 1.8984375
- router: bfloat16 [6144, 4], replicated, may hold values from -0.078125 to 0.078125
- routes: int32 [192, 2], P(('groups', 'expert')), parts along dimension 0, may hold values from 0 to 3, all different within a row; in each aligned block of 6 rows (0 to 5, 6 to 11, ...) at most 4 rows name the same one
- gate_weight: bfloat16 [6144, 32768], P(None, 'expert'), may hold values from -0.078125 to 0.078125
- up_weight: bfloat16 [6144, 32768], P(None, 'expert'), may hold values from -0.078125 to 0.078125
- down_weight: bfloat16 [32768, 6144], P('expert'), may hold values from -0.0625 to 0.0625
- accepted: int32 [32], P(('groups', 'expert')), parts along dimension 0, may hold values from 0 to 5
- next_embed: bfloat16 [32, 6144], P(('groups', 'expert')), parts along dimension 0, may hold values from -6 to 6
- draft_fc: bfloat16 [12288, 6144], P('expert'), may hold values from -0.0546875 to 0.0546875
Outputs:
- layer_out: bfloat16 [192, 6144], P(('groups', 'expert')), parts along dimension 0
- draft_out: bfloat16 [32, 6144], P(('groups', 'expert')), parts along dimension 0
There are 2 independent parts, one for each index of `groups`. A program takes and returns all parts, laid end to end along the dimension named above; an argument that names none is the same for every part. Nothing has to cross between parts.
Inputs may be any that keep to these rules, and one draw needn't show every extreme that they name: `lengths`: both ends are reached by some request. `parents`: entry i of a request's 6 entries names an earlier node as its parent; entry 0, the root, names itself. `routes`: among the rows of one device no expert is named more than 4 times, a bound that some block reaches.
All inputs are finite; a program needn't handle non-finite values.
Results may differ from a plain program's by a relative error of at most 0.0051.
Values may be sent and summed in bfloat16 or wider, within the bound.
A program may use at most 128 MiB of HBM per device.

v0:
```python
import functools

import jax
import jax.numpy as jnp
from jax import lax
from jax.experimental import pallas as pl
from jax.experimental.pallas import tpu as pltpu
from jax.sharding import PartitionSpec as P

QUERY_HEADS = 48
KEY_VALUE_HEADS = 8
HEAD_SIZE = 128
EXPERTS = 4
TREE_NODES = 6
CACHE_SLOTS = 512
CAP = 4


EPSILON = 1e-05


def related_kernel(parents, out):
    node_ids = lax.broadcasted_iota(jnp.int32, (1, out.shape[2]), 1)
    for request in range(out.shape[0]):
        reached = []
        for node in range(TREE_NODES):
            row = (node_ids == node).astype(jnp.float32)
            parent = parents[request * TREE_NODES + node]
            for earlier in range(node):
                row = row + jnp.where(parent == earlier, reached[earlier], 0.0)
            reached.append(row)
            out[request, node : node + 1, :] = row


def ancestors(parent_ids):
    table = pl.pallas_call(
        related_kernel,
        out_shape=jax.ShapeDtypeStruct((parent_ids.shape[0] // TREE_NODES, TREE_NODES, 128), jnp.float32),
        in_specs=[pl.BlockSpec(memory_space=pltpu.SMEM)],
        out_specs=pl.BlockSpec(memory_space=pltpu.VMEM),
        name="related",
    )(parent_ids)
    return table[:, :, :TREE_NODES] > 0.5


def attention(queries, tree_key_value, key_value_cache, lengths, parents):
    request_total = lengths.shape[0]
    query_head_count = queries.reshape(
        request_total, TREE_NODES, KEY_VALUE_HEADS, QUERY_HEADS // KEY_VALUE_HEADS, HEAD_SIZE
    )
    cached_key_rows = key_value_cache[:, 0].reshape(
        request_total, CACHE_SLOTS, KEY_VALUE_HEADS, HEAD_SIZE
    )
    cached_value_rows = key_value_cache[:, 1].reshape(
        request_total, CACHE_SLOTS, KEY_VALUE_HEADS, HEAD_SIZE
    )
    tree_key_rows = tree_key_value[:, 0].reshape(
        request_total, TREE_NODES, KEY_VALUE_HEADS, HEAD_SIZE
    )
    tree_value_rows = tree_key_value[:, 1].reshape(
        request_total, TREE_NODES, KEY_VALUE_HEADS, HEAD_SIZE
    )
    score_scale = HEAD_SIZE ** (-0.5)
    cache_scores = (
        jnp.einsum(
            "rtgqd,rlgd->rgtql",
            query_head_count,
            cached_key_rows,
            preferred_element_type=jnp.float32,
        )
        * score_scale
    )
    tree_scores = (
        jnp.einsum(
            "rtgqd,rugd->rgtqu", query_head_count, tree_key_rows, preferred_element_type=jnp.float32
        )
        * score_scale
    )
    visible = jnp.arange(CACHE_SLOTS, dtype=jnp.int32)[None, :] < lengths[:, None]
    related = ancestors(parents)
    cache_scores = jnp.where(visible[:, None, None, None, :], cache_scores, -1e30)
    tree_scores = jnp.where(related[:, None, :, None, :], tree_scores, -1e30)
    row_peak = jnp.maximum(jnp.max(cache_scores, axis=-1), jnp.max(tree_scores, axis=-1))[..., None]
    cache_exp = jnp.exp(cache_scores - row_peak)
    tree_exp = jnp.exp(tree_scores - row_peak)
    denominator = (jnp.sum(cache_exp, axis=-1) + jnp.sum(tree_exp, axis=-1))[..., None]
    cache_weights = (cache_exp / denominator).astype(jnp.bfloat16)
    tree_weights = (tree_exp / denominator).astype(jnp.bfloat16)
    context = jnp.einsum(
        "rgtql,rlgd->rtgqd", cache_weights, cached_value_rows, preferred_element_type=jnp.float32
    ) + jnp.einsum(
        "rgtqu,rugd->rtgqd", tree_weights, tree_value_rows, preferred_element_type=jnp.float32
    )
    return context.reshape(request_total * TREE_NODES, QUERY_HEADS * HEAD_SIZE)


VMEM_LIMIT = 66_000_000


def greet(n, me):
    barrier = pltpu.get_barrier_semaphore()

    def hello(k, carry):
        pl.semaphore_signal(barrier, inc=1, device_id={"expert": lax.rem(me + k, n)})
        return carry

    lax.fori_loop(1, n, hello, 0)
    pl.semaphore_wait(barrier, n - 1)


def push(src, dst, send_sem, recv_sem, peer):
    return pltpu.make_async_remote_copy(
        src_ref=src,
        dst_ref=dst,
        send_sem=send_sem,
        recv_sem=recv_sem,
        device_id={"expert": peer},
        device_id_type=pl.DeviceIdType.MESH,
    )


def moe_kernel(
    n,
    group_size,
    pair_slots,
    down_slots,
    packed,
    gate_hbm,
    up_hbm,
    down_hbm,
    grouped,
    gate_buf,
    up_buf,
    down_buf,
    arrived,
    rows_wide,
    rows,
    activation,
    result,
    leaving,
    returned,
    pair_sem,
    down_sem,
    out_sem,
    in_sem,
    back_out_sem,
    back_in_sem,
    own_sem,
):
    me = lax.axis_index("expert")
    width = gate_hbm.shape[1]
    chunk = gate_buf.shape[2]
    pair_count = width // chunk
    piece = down_buf.shape[2]
    piece_count = down_hbm.shape[1] // piece

    def pair_copies(i):
        slot = lax.rem(i, pair_slots)
        cols = pl.ds(pl.multiple_of(i * chunk, chunk), chunk)
        return (
            pltpu.make_async_copy(gate_hbm.at[:, cols], gate_buf.at[slot], pair_sem.at[0, slot]),
            pltpu.make_async_copy(up_hbm.at[:, cols], up_buf.at[slot], pair_sem.at[1, slot]),
        )

    def down_copy(i):
        slot = lax.rem(i, down_slots)
        cols = pl.ds(pl.multiple_of(i * piece, piece), piece)
        return pltpu.make_async_copy(down_hbm.at[:, cols], down_buf.at[slot], down_sem.at[slot])

    def start_pair(i, carry):
        for copy in pair_copies(i):
            copy.start()
        return carry

    def start_down(i, carry):
        down_copy(i).start()
        return carry

    lax.fori_loop(0, pair_slots, start_pair, 0)
    greet(n, me)

    def dispatch(k, carry):
        peer = lax.rem(me + k, n)
        push(
            packed.at[peer // group_size], arrived.at[me], out_sem.at[peer], in_sem.at[me], peer
        ).start()
        return carry

    lax.fori_loop(1, n, dispatch, 0)
    own = pltpu.make_async_copy(packed.at[me // group_size], arrived.at[me], own_sem)
    own.start()
    lax.fori_loop(0, down_slots, start_down, 0)
    own.wait()

    def take(k, carry):
        source = lax.rem(me + n - k, n)
        push(
            packed.at[0], arrived.at[source], out_sem.at[source], in_sem.at[source], source
        ).wait_recv()
        return carry

    lax.fori_loop(1, n, take, 0)

    def both(pair):
        return pl.ds(pl.multiple_of(pair * 2 * CAP, 2 * CAP), 2 * CAP)

    def widen(pair, carry):
        rows_wide[both(pair), :] = jnp.concatenate(
            [arrived[2 * pair].astype(jnp.float32), arrived[2 * pair + 1].astype(jnp.float32)],
            axis=0,
        )
        return carry

    lax.fori_loop(0, n // 2, widen, 0)
    rows[...] = rows_wide[...].astype(jnp.bfloat16)

    def pair_step(i, carry):
        slot = lax.rem(i, pair_slots)
        for copy in pair_copies(i):
            copy.wait()
        gate_val = jnp.dot(rows[...], gate_buf[slot], preferred_element_type=jnp.float32)
        up_val = jnp.dot(rows[...], up_buf[slot], preferred_element_type=jnp.float32)
        cols = pl.ds(pl.multiple_of(i * chunk, chunk), chunk)
        activation[:, cols] = (jax.nn.silu(gate_val) * up_val).astype(jnp.bfloat16)

        @pl.when(i + pair_slots < pair_count)
        def _():
            start_pair(i + pair_slots, 0)

        return carry

    lax.fori_loop(0, pair_count, pair_step, 0)

    def down_step(i, carry):
        slot = lax.rem(i, down_slots)
        down_copy(i).wait()
        result[...] = jnp.dot(
            activation[...], down_buf[slot], preferred_element_type=jnp.float32
        )

        @pl.when(i + down_slots < piece_count)
        def _():
            start_down(i + down_slots, 0)

        def narrow(pair, inner):
            block = result[both(pair), :]
            leaving[2 * pair, i] = block[:CAP].astype(jnp.bfloat16)
            leaving[2 * pair + 1, i] = block[CAP:].astype(jnp.bfloat16)
            return inner

        lax.fori_loop(0, n // 2, narrow, 0)

        def send_back(k, inner):
            peer = lax.rem(me + k, n)
            push(
                leaving.at[peer, i],
                returned.at[me, i],
                back_out_sem.at[peer],
                back_in_sem.at[me],
                peer,
            ).start()
            return inner

        lax.fori_loop(1, n, send_back, 0)
        return carry

    lax.fori_loop(0, piece_count, down_step, 0)
    returned[me] = leaving[me]

    def drain(k, carry):
        peer = lax.rem(me + n - k, n)
        push(
            leaving.at[peer], returned.at[peer], back_out_sem.at[peer], back_in_sem.at[peer], peer
        ).wait()
        push(
            packed.at[0], arrived.at[peer], out_sem.at[peer], in_sem.at[peer], peer
        ).wait_send()
        return carry

    lax.fori_loop(1, n, drain, 0)

    def gather(expert, carry):
        for i in range(piece_count):

            def add(member, total):
                return total + returned[expert * group_size + member, i].astype(jnp.float32)

            grouped[expert, :, i * piece : (i + 1) * piece] = lax.fori_loop(
                0, group_size, add, jnp.zeros((CAP, piece), jnp.float32)
            )
        return carry

    lax.fori_loop(0, EXPERTS, gather, 0)


def moe(packed, gate_weight, up_weight, down_weight, n):
    model_width, width = gate_weight.shape
    row_count = n * CAP
    chunk = min(512, width)
    piece = model_width // 4
    pair_slots = min(3, width // chunk)
    down_slots = min(2, model_width // piece)
    anywhere = pl.BlockSpec(memory_space=pl.ANY)
    whole = pl.BlockSpec(memory_space=pltpu.VMEM)
    bf16, f32 = jnp.bfloat16, jnp.float32
    return pl.pallas_call(
        functools.partial(moe_kernel, n, n // EXPERTS, pair_slots, down_slots),
        out_shape=jax.ShapeDtypeStruct((EXPERTS, CAP, model_width), f32),
        in_specs=[whole, anywhere, anywhere, anywhere],
        out_specs=whole,
        scratch_shapes=[
            pltpu.VMEM((pair_slots, model_width, chunk), bf16),
            pltpu.VMEM((pair_slots, model_width, chunk), bf16),
            pltpu.VMEM((down_slots, width, piece), bf16),
            pltpu.VMEM((n, CAP, model_width), bf16),
            pltpu.VMEM((row_count, model_width), f32),
            pltpu.VMEM((row_count, model_width), bf16),
            pltpu.VMEM((row_count, width), bf16),
            pltpu.VMEM((row_count, piece), f32),
            pltpu.VMEM((n, model_width // piece, CAP, piece), bf16),
            pltpu.VMEM((n, model_width // piece, CAP, piece), bf16),
            pltpu.SemaphoreType.DMA((2, pair_slots)),
            pltpu.SemaphoreType.DMA((down_slots,)),
            pltpu.SemaphoreType.DMA((n,)),
            pltpu.SemaphoreType.DMA((n,)),
            pltpu.SemaphoreType.DMA((n,)),
            pltpu.SemaphoreType.DMA((n,)),
            pltpu.SemaphoreType.DMA,
        ],
        compiler_params=pltpu.CompilerParams(
            collective_id=0, has_side_effects=True, vmem_limit_bytes=VMEM_LIMIT
        ),
        name="moe",
    )(packed, gate_weight, up_weight, down_weight)


def draft_kernel(
    n,
    share,
    piece,
    blocks,
    fc_hbm,
    out,
    fc_buf,
    arrived,
    rows_wide,
    result,
    leaving,
    returned,
    fc_sem,
    out_sem,
    in_sem,
    back_out_sem,
    back_in_sem,
):
    me = lax.axis_index("expert")
    piece_count = fc_hbm.shape[1] // piece
    half = piece // 2

    def fc_copy(i):
        cols = pl.ds(pl.multiple_of(i * piece, piece), piece)
        return pltpu.make_async_copy(fc_hbm.at[:, cols], fc_buf.at[i], fc_sem.at[i])

    def start_fc(i, carry):
        fc_copy(i).start()
        return carry

    lax.fori_loop(0, piece_count, start_fc, 0)
    greet(n, me)

    def dispatch(k, carry):
        peer = lax.rem(me + k, n)
        push(blocks.at[peer], arrived.at[me], out_sem.at[peer], in_sem.at[me], peer).start()
        return carry

    lax.fori_loop(1, n, dispatch, 0)
    rows_wide[pl.ds(me * share, share), :] = blocks[me]

    def take(k, carry):
        source = lax.rem(me + n - k, n)
        push(
            blocks.at[source], arrived.at[source], out_sem.at[source], in_sem.at[source], source
        ).wait()
        rows_wide[pl.ds(source * share, share), :] = arrived[source]
        return carry

    lax.fori_loop(1, n, take, 0)

    def step(i, carry):
        fc_copy(i).wait()
        result[...] = jnp.dot(
            rows_wide[...].astype(jnp.bfloat16), fc_buf[i], preferred_element_type=jnp.float32
        )

        def split(source, inner):
            block = result[pl.ds(source * share, share), :]
            leaving[source, i] = jnp.concatenate(
                [block[:, :half], block[:, half:]], axis=0
            ).astype(jnp.bfloat16)
            return inner

        lax.fori_loop(0, n, split, 0)

        def send_back(k, inner):
            peer = lax.rem(me + k, n)
            push(
                leaving.at[peer, i],
                returned.at[me, i],
                back_out_sem.at[peer],
                back_in_sem.at[me],
                peer,
            ).start()
            return inner

        lax.fori_loop(1, n, send_back, 0)
        return carry

    lax.fori_loop(0, piece_count, step, 0)
    returned[me] = leaving[me]

    def drain(k, carry):
        peer = lax.rem(me + n - k, n)
        push(
            leaving.at[peer], returned.at[peer], back_out_sem.at[peer], back_in_sem.at[peer], peer
        ).wait()
        return carry

    lax.fori_loop(1, n, drain, 0)
    for i in range(piece_count):

        def add(source, total):
            return total + returned[source, i].astype(jnp.float32)

        total = lax.fori_loop(0, n, add, jnp.zeros((2 * share, half), jnp.float32))
        out[:, i * piece : i * piece + half] = total[:share]
        out[:, i * piece + half : (i + 1) * piece] = total[share:]


def draft(blocks, draft_fc):
    n, share, depth = blocks.shape
    model_width = draft_fc.shape[1]
    piece = model_width // 4
    pieces = model_width // piece
    whole = pl.BlockSpec(memory_space=pltpu.VMEM)
    f32 = jnp.float32
    return pl.pallas_call(
        functools.partial(draft_kernel, n, share, piece),
        out_shape=jax.ShapeDtypeStruct((share, model_width), f32),
        in_specs=[whole, pl.BlockSpec(memory_space=pl.ANY)],
        out_specs=whole,
        scratch_shapes=[
            pltpu.VMEM((pieces, depth, piece), jnp.bfloat16),
            pltpu.VMEM((n, share, depth), f32),
            pltpu.VMEM((n * share, depth), f32),
            pltpu.VMEM((n * share, piece), f32),
            pltpu.VMEM((n, pieces, 2 * share, piece // 2), jnp.bfloat16),
            pltpu.VMEM((n, pieces, 2 * share, piece // 2), jnp.bfloat16),
            pltpu.SemaphoreType.DMA((pieces,)),
            pltpu.SemaphoreType.DMA((n,)),
            pltpu.SemaphoreType.DMA((n,)),
            pltpu.SemaphoreType.DMA((n,)),
            pltpu.SemaphoreType.DMA((n,)),
        ],
        compiler_params=pltpu.CompilerParams(
            collective_id=1, has_side_effects=True, vmem_limit_bytes=VMEM_LIMIT
        ),
        name="draft",
    )(blocks, draft_fc)


def per_device(
    queries,
    tree_key_value,
    key_value_cache,
    lengths,
    parents,
    residual,
    ffn_gain,
    router,
    routes,
    gate_weight,
    up_weight,
    down_weight,
    accepted,
    next_embed,
    draft_fc,
):
    devices = lax.axis_size("expert")
    context = attention(queries, tree_key_value, key_value_cache, lengths, parents)
    hidden_state = residual.astype(jnp.float32) + context
    normed = (
        hidden_state
        * lax.rsqrt(jnp.mean(hidden_state * hidden_state, axis=-1, keepdims=True) + EPSILON)
        * ffn_gain.astype(jnp.float32)
    ).astype(jnp.bfloat16)
    tokens_here, model_width = normed.shape
    logits = jnp.dot(normed, router, preferred_element_type=jnp.float32)
    expert_ids = jnp.arange(EXPERTS, dtype=jnp.int32)
    first_hit = (routes[:, 0:1] == expert_ids[None, :]).astype(jnp.float32)
    second_hit = (routes[:, 1:2] == expert_ids[None, :]).astype(jnp.float32)
    first_logit = jnp.sum(logits * first_hit, axis=-1)
    second_logit = jnp.sum(logits * second_hit, axis=-1)
    first_share = jax.nn.sigmoid(first_logit - second_logit)
    mixing = first_share[:, None] * first_hit + (1.0 - first_share)[:, None] * second_hit
    hit_table = first_hit + second_hit
    slot_rank = jnp.cumsum(hit_table, axis=0) - 1.0
    slot_ids = jnp.arange(CAP, dtype=jnp.float32)
    placing = hit_table.T[:, None, :] * (slot_rank.T[:, None, :] == slot_ids[None, :, None]).astype(
        jnp.float32
    )
    packed = jnp.einsum(
        "ect,td->ecd", placing.astype(jnp.bfloat16), normed, preferred_element_type=jnp.float32
    ).astype(jnp.bfloat16)
    grouped = moe(packed, gate_weight, up_weight, down_weight, devices)
    weighted = placing * mixing.T[:, None, :]
    expert_sum = jnp.einsum("ect,ecd->td", weighted, grouped, precision=lax.Precision.HIGHEST)
    layer_out = (hidden_state + expert_sum).astype(jnp.bfloat16)
    request_total = lengths.shape[0]
    picker = (accepted[:, None] == jnp.arange(TREE_NODES, dtype=jnp.int32)[None, :]).astype(
        jnp.bfloat16
    )
    picked = jnp.einsum(
        "rt,rtd->rd",
        picker,
        layer_out.reshape(request_total, TREE_NODES, model_width),
        preferred_element_type=jnp.float32,
    ).astype(jnp.bfloat16)
    draft_in = jnp.concatenate([picked, next_embed], axis=1)
    depth = draft_fc.shape[0]
    blocks = draft_in.reshape(request_total, devices, depth).transpose(1, 0, 2)
    draft_out = draft(blocks.astype(jnp.float32), draft_fc).astype(jnp.bfloat16)
    return (layer_out, draft_out)


def solution(mesh):
    return jax.shard_map(
        per_device,
        mesh=mesh,
        in_specs=(
            P(("groups", "expert"), None),
            P(("groups", "expert"), None, None),
            P(("groups", "expert"), None, None, None),
            P(("groups", "expert")),
            P(("groups", "expert")),
            P(("groups", "expert"), None),
            P(),
            P(),
            P(("groups", "expert"), None),
            P(None, "expert"),
            P(None, "expert"),
            P("expert", None),
            P(("groups", "expert")),
            P(("groups", "expert"), None),
            P("expert", None),
        ),
        out_specs=(P(("groups", "expert"), None), P(("groups", "expert"), None)),
        check_vma=False,
    )
```

profile of v0, /device:TPU:0, one launch (start us, length us, event | category | flops | bytes accessed | tf_op | source)
XLA Modules:
  0.0 90.7 jit_solution(3661812183383402705)
XLA Ops:
  0.6 1.7 %fusion.28 = (bf16[1,1,512,1024]{3,2,1,0:T(8,128)(2,1)S(1)}, bf16[1,1,512,1024]{3,2,1,0:T(8,128)(2,1)S(1)}) fusion(bf16[1,2,512,1024]{3,2,1,0:T(8,128)(2,1)} %param.17), kind=kLoop, calls=%fused_computation.65 | loop fusion | bytes 4194304 | tf_op jit(solution)/shard_map/slice | solution.py:54
  2.4 0.5 copy.46
  2.9 1.0 %reshape.253 = bf16[6,8,6,128]{3,2,1,0:T(8,128)(2,1)S(1)} reshape(bf16[6,6144]{1,0:T(8,128)(2,1)} %param.15) | data formatting | bytes 147456 | tf_op jit(solution)/shard_map/reshape.2
  4.6 0.4 fusion.29
  5.0 0.9 %slice_reduce_fusion = (bf16[6,1024]{1,0:T(8,128)(2,1)S(1)}, bf16[6,1024]{1,0:T(8,128)(2,1)S(1)}) fusion(bf16[6,2,1024]{2,1,0:T(2,128)(2,1)} %param.16), kind=kLoop, calls=%fused_computation.27 | loop fusion | bytes 49152 | tf_op jit(solution)/shard_map/slice | solution.py:60
  5.9 1.3 %related.1 = f32[1,6,128]{2,1,0:T(8,128)} custom-call(s32[6]{0:T(128)} %parents.1), custom_call_target="tpu_custom_call" | custom-call | tf_op jit(solution)/shard_map/related/pallas_call | solution.py:36
  7.2 0.7 fusion.21
  7.9 0.6 fusion.30
  8.6 0.3 fusion.5
  8.9 0.2 fusion.11
  9.1 0.5 copy.47
  9.7 0.5 fusion.4
  10.3 1.1 %multiply_reduce_fusion = f32[6]{0:T(128)S(1)} fusion(f32[6,6144]{1,0:T(8,128)S(1)} %reshape.258, bf16[6,6144]{1,0:T(8,128)(2,1)} %param.20), kind=kLoop, calls=%fused_computation.17 | loop fusion | flops 147450 | bytes 221208 | tf_op jit(solution)/shard_map/reduce_sum | solution.py:493
  11.4 0.7 convert_element_type.69
  12.1 1.0 %multiply_convert_fusion = bf16[6,6144]{1,0:T(8,128)(2,1)S(1)} fusion(f32[6144]{0:T(1024)S(1)} %convert_element_type.69, f32[6]{0:T(128)S(1)} %add_rsqrt_fusion, f32[6,6144]{1,0:T(8,128)S(1)} %reshape.258, bf16[6,6144]{1,0:T(8,128)(2,1)} %param.20), kind=kLoop, calls=%fused_computation.16 | loop fusion | flops 184320 | bytes 319512 | tf_op jit(solution)/shard_map/convert_element_type | solution.py:495
  13.1 0.8 slice_bitcast_fusion.1
  13.8 0.2 select_reduce_fusion
  14.0 0.2 reduce_window_sum.11
  14.2 0.9 convolution_convert_fusion.packed
  15.1 52.0 %moe.1 = f32[4,4,6144]{2,1,0:T(4,128)} custom-call(bf16[4,4,6144]{2,1,0:T(4,128)(2,1)} %convolution_convert_fusion.packed, bf16[6144,2048]{1,0:T(8,128)(2,1)} %gate_hbm.1, bf16[6144,2048]{1,0:T(8,128)(2,1)} %up_hbm.1, bf16[2048,6144]{1,0:T(8,128)(2,1)} %down_hbm.1), custom_call_target="tpu_custom_call" | custom-call | tf_op jit(solution)/shard_map/moe/pallas_call | solution.py:306
  67.2 1.9 %fusion.1 = bf16[6,6144]{1,0:T(8,128)(2,1)S(1)} fusion(f32[4,4,6144]{2,1,0:T(4,128)} %moe.1, f32[6,6144]{1,0:T(8,128)S(1)} %reshape.258, bf16[6,6144]{1,0:T(8,128)(2,1)S(1)} %copy-done.1, f32[4,6]{1,0:T(4,128)S(1)} %get-tuple-element.10, f32[4,6]{1,0:T(4,128)S(1)} %get-tuple-element.11, f32[4,6]{1,0:T(4,128)S(1)} %add_bitcast_fusion), kind=kOutput, calls=%fused_computation.3 | convolution fusion | flops 7225632 | bytes 688416 | tf_op jit(solution)/shard_map/ect,ecd->td/dot_general | solution.py:516
  70.0 0.7 convert.1.blocks
  70.6 18.7 %draft.1 = f32[1,6144]{1,0:T(1,128)} custom-call(f32[16,1,768]{2,1,0:T(1,128)} %convert.1.blocks, bf16[768,6144]{1,0:T(8,128)(2,1)} %fc_hbm.1), custom_call_target="tpu_custom_call" | custom-call | tf_op jit(solution)/shard_map/draft/pallas_call | solution.py:446
  89.4 1.4 %convert_element_type.78 = bf16[1,6144]{1,0:T(2,128)(2,1)} convert(f32[1,6144]{1,0:T(1,128)} %draft.1) | non-fusion elementwise | flops 6144 | bytes 36864 | tf_op jit(solution)/shard_map/convert_element_type | solution.py:531
  (25 shorter events, 0.5 us)
Async XLA Ops:
  0.6 13.2 %copy-start = (bf16[6144,4]{0,1:T(4,128)(2,1)S(1)}, bf16[6144,4]{0,1:T(4,128)(2,1)}, u32[]{:S(2)}) copy-start(bf16[6144,4]{0,1:T(4,128)(2,1)} %param.22) | copy-start | bytes 147460
  15.1 52.0 %copy-start.1 = (bf16[6,6144]{1,0:T(8,128)(2,1)S(1)}, bf16[6,6144]{1,0:T(8,128)(2,1)}, u32[]{:S(2)}) copy-start(bf16[6,6144]{1,0:T(8,128)(2,1)} %param.20) | copy-start | bytes 221188
  15.1 54.8 %copy-start.3 = (bf16[1,6144]{1,0:T(2,128)(2,1)S(1)}, bf16[1,6144]{1,0:T(2,128)(2,1)}, u32[]{:S(2)}) copy-start(bf16[1,6144]{1,0:T(2,128)(2,1)} %param.28) | copy-start | bytes 36868
  69.0 21.7 %copy-start.2 = (bf16[6,6144]{1,0:T(8,128)(2,1)}, bf16[6,6144]{1,0:T(8,128)(2,1)S(1)}, u32[]{:S(2)}) copy-start(bf16[6,6144]{1,0:T(8,128)(2,1)S(1)} %fusion.1) | copy-start | bytes 221188
where the time goes:
time: 91.4 us; the launch traced here: 90.7 us
  Pallas kernels  72 us (79%)
  other arithmetic  6.17 us (7%)
  local copies, waits for them, and re-layouts  5.61 us (6%)
  matrix products  4.79 us (5%)
  between operations  2.13 us (2%)
    pallas_call x1, Pallas kernels, moe(): pl.pallas_call(functools.partial(moe_kernel, n, n // EXPERTS, pair_slots,...  52 us
    pallas_call x1, Pallas kernels, draft(): pl.pallas_call(functools.partial(draft_kernel, n, share, piece), out_shap...  18.7 us
    convert_element_type x2, other arithmetic, per_device(): draft_out = draft(blocks.astype(jnp.float32), draft_fc).astype(jnp.bfloat16)  2.03 us
    dot_general x1, matrix products, per_device(): jnp.einsum('ect,ecd->td', weighted, grouped, precision=lax.Precision.HIGH...  1.88 us

commit v1 on v0

--- a/solution.py
+++ b/solution.py
@@ -468,6 +468,697 @@
     )(blocks, draft_fc)
 
 
+SLICE = 1024
+
+
+def greet_all(n, me):
+    barrier = pltpu.get_barrier_semaphore()
+
+    def hello(k, carry):
+        pl.semaphore_signal(barrier, inc=1, device_id={"expert": lax.rem(me + k, n)})
+        return carry
+
+    lax.fori_loop(1, n, hello, 0)
+    return barrier
+
+
+def fused_kernel(
+    n,
+    slots,
+    lengths,
+    parents,
+    routes,
+    accepted,
+    queries_hbm,
+    tree_hbm,
+    cache_hbm,
+    residual_hbm,
+    gain_hbm,
+    router_hbm,
+    embed_hbm,
+    gate_hbm,
+    up_hbm,
+    down_hbm,
+    fc_hbm,
+    layer_out,
+    draft_out,
+    weights,
+    queries,
+    tree,
+    keys,
+    values,
+    residual,
+    gain,
+    router,
+    embed,
+    tree_rows,
+    hidden,
+    normed,
+    packed,
+    arrived,
+    rows,
+    gate_sum,
+    up_sum,
+    activation,
+    leaving,
+    returned,
+    home_leaving,
+    home_returned,
+    picked,
+    embed_row,
+    blocks,
+    block_rows,
+    draft_leaving,
+    draft_returned,
+    load_sem,
+    input_sem,
+    out_sem,
+    in_sem,
+    plane_out_sem,
+    plane_in_sem,
+    back_out_sem,
+    back_in_sem,
+    home_out_sem,
+    home_in_sem,
+    block_out_sem,
+    block_in_sem,
+    draft_out_sem,
+    draft_in_sem,
+):
+    bf16, f32 = jnp.bfloat16, jnp.float32
+    me = lax.axis_index("expert")
+    group = n // EXPERTS
+    mine = me // group
+    lane = lax.rem(me, group)
+    model_width = down_hbm.shape[1]
+    width = down_hbm.shape[0]
+    depth = fc_hbm.shape[0]
+    chunk_count = model_width // width
+    half_count = width // SLICE
+    piece_count = model_width // SLICE
+    stacked = width // depth
+    pair_loads = 2 * chunk_count * half_count
+    down_loads = pair_loads + piece_count
+    load_count = down_loads + -(-piece_count // stacked)
+    block_count = model_width // depth
+    half = SLICE // 2
+    padded = 8
+    share = EXPERTS * CAP
+    cache_slots = cache_hbm.shape[2]
+    key_rows = keys.shape[0]
+
+    def fc_copy(p):
+        i, part = down_loads + p // stacked, p % stacked
+        return pltpu.make_async_copy(
+            fc_hbm.at[:, p * SLICE : (p + 1) * SLICE],
+            weights.at[i % slots, part * depth : (part + 1) * depth, :],
+            load_sem.at[i, part],
+        )
+
+    def load_copies(i):
+        slot = weights.at[i % slots]
+        if i < pair_loads:
+            source = gate_hbm if i % 2 == 0 else up_hbm
+            k, h = i // (2 * half_count), i // 2 % half_count
+            view = source.at[k * width : (k + 1) * width, h * SLICE : (h + 1) * SLICE]
+            return [pltpu.make_async_copy(view, slot, load_sem.at[i, 0])]
+        if i < down_loads:
+            p = i - pair_loads
+            view = down_hbm.at[:, p * SLICE : (p + 1) * SLICE]
+            return [pltpu.make_async_copy(view, slot, load_sem.at[i, 0])]
+        first = (i - down_loads) * stacked
+        return [fc_copy(p) for p in range(first, min(first + stacked, piece_count))]
+
+    def start_load(i):
+        if i < load_count:
+            for copy in load_copies(i):
+                copy.start()
+
+    inputs = [
+        pltpu.make_async_copy(source, target, input_sem.at[i])
+        for i, (source, target) in enumerate(
+            [
+                (queries_hbm, queries),
+                (tree_hbm, tree),
+                (cache_hbm.at[0, 0], keys.at[0:cache_slots, :]),
+                (residual_hbm, residual),
+                (cache_hbm.at[0, 1], values.at[0:cache_slots, :]),
+                (gain_hbm, gain),
+                (router_hbm, router),
+                (embed_hbm, embed),
+            ]
+        )
+    ]
+    for copy in inputs:
+        copy.start()
+    for i in range(slots):
+        start_load(i)
+    barrier = greet_all(n, me)
+
+    row8 = lax.broadcasted_iota(jnp.int32, (padded, 128), 0)
+    col8 = lax.broadcasted_iota(jnp.int32, (padded, 128), 1)
+    node_ids = lax.broadcasted_iota(jnp.int32, (1, 128), 1)
+    reached = []
+    related = jnp.zeros((padded, 128), f32)
+    for node in range(TREE_NODES):
+        row = (node_ids == node).astype(f32)
+        parent = parents[node]
+        for earlier in range(node):
+            row = row + jnp.where(parent == earlier, reached[earlier], 0.0)
+        reached.append(row)
+        related = related + jnp.where(row8 == node, row, 0.0)
+    slot_ids = lax.broadcasted_iota(jnp.int32, (padded, cache_slots), 1)
+    bias = jnp.concatenate(
+        [
+            jnp.where(slot_ids < lengths[0], 0.0, -1e30),
+            jnp.where(related > 0.5, 0.0, -1e30),
+        ],
+        axis=1,
+    )
+    heads_each = QUERY_HEADS // KEY_VALUE_HEADS
+    bias = jnp.concatenate([bias] * heads_each, axis=0)
+
+    def named(choice, token):
+        expert = routes[choice, token]
+        rank = jnp.int32(0)
+        for earlier in range(token):
+            for other in range(2):
+                rank = rank + jnp.where(routes[other, earlier] == expert, 1, 0)
+        return expert, rank
+
+    places = [[named(choice, token) for choice in range(2)] for token in range(TREE_NODES)]
+
+    for copy in inputs[:3]:
+        copy.wait()
+    tree_rows[...] = jnp.zeros_like(tree_rows)
+    for token in range(TREE_NODES):
+        both = tree[token].astype(f32)
+        tree_rows[0, token : token + 1, :] = both[0:1]
+        tree_rows[1, token : token + 1, :] = both[1:2]
+    tile = tree_rows.shape[1]
+    keys[cache_slots : cache_slots + tile, :] = tree_rows[0].astype(bf16)
+    keys[cache_slots + tile :, :] = jnp.zeros((key_rows - cache_slots - tile, keys.shape[1]), bf16)
+    values[cache_slots : cache_slots + tile, :] = tree_rows[1].astype(bf16)
+    values[cache_slots + tile :, :] = jnp.zeros(
+        (key_rows - cache_slots - tile, keys.shape[1]), bf16
+    )
+    spare = jnp.zeros((padded - TREE_NODES, HEAD_SIZE), f32)
+    score_scale = HEAD_SIZE ** (-0.5)
+    weights_of = []
+    for g in range(KEY_VALUE_HEADS):
+        parts = []
+        for q in range(heads_each):
+            head = g * heads_each + q
+            parts.append(queries[:, head * HEAD_SIZE : (head + 1) * HEAD_SIZE].astype(f32))
+            parts.append(spare)
+        head_queries = jnp.concatenate(parts, axis=0).astype(bf16)
+        scores = (
+            lax.dot_general(
+                head_queries,
+                keys[:, g * HEAD_SIZE : (g + 1) * HEAD_SIZE],
+                (((1,), (1,)), ((), ())),
+                preferred_element_type=f32,
+            )
+            * score_scale
+            + bias
+        )
+        peak = jnp.max(scores, axis=-1, keepdims=True)
+        grown = jnp.exp(scores - peak)
+        total = jnp.sum(grown, axis=-1, keepdims=True)
+        weights_of.append((grown * (1.0 / total)).astype(bf16))
+    for copy in inputs[3:5]:
+        copy.wait()
+    square = jnp.zeros((padded, HEAD_SIZE), f32)
+    for g in range(KEY_VALUE_HEADS):
+        context = jnp.dot(
+            weights_of[g],
+            values[:, g * HEAD_SIZE : (g + 1) * HEAD_SIZE],
+            preferred_element_type=f32,
+        )
+        for q in range(heads_each):
+            head = g * heads_each + q
+            cols = slice(head * HEAD_SIZE, (head + 1) * HEAD_SIZE)
+            state = context[q * padded : (q + 1) * padded] + jnp.concatenate(
+                [residual[:, cols].astype(f32), spare], axis=0
+            )
+            hidden[:, cols] = state
+            square = square + state * state
+    for copy in inputs[5:]:
+        copy.wait()
+    level = lax.rsqrt(jnp.sum(square, axis=-1, keepdims=True) / model_width + EPSILON)
+
+    slot_row = lax.broadcasted_iota(jnp.int32, (EXPERTS * padded, padded), 0)
+    slot_col = lax.broadcasted_iota(jnp.int32, (EXPERTS * padded, padded), 1)
+    placing = jnp.zeros((EXPERTS * padded, padded), f32)
+    for token, choices in enumerate(places):
+        for expert, rank in choices:
+            placing = placing + jnp.where(
+                (slot_row == expert * padded + rank) & (slot_col == token), 1.0, 0.0
+            )
+    placing = placing.astype(bf16)
+
+    pl.semaphore_wait(barrier, n - 1)
+
+    def push(src, dst, send_sem, recv_sem, peer):
+        return pltpu.make_async_remote_copy(
+            src_ref=src,
+            dst_ref=dst,
+            send_sem=send_sem,
+            recv_sem=recv_sem,
+            device_id={"expert": peer},
+            device_id_type=pl.DeviceIdType.MESH,
+        )
+
+    def to_plane(k, step):
+        peer_plane = lax.rem(mine + step, EXPERTS)
+        return push(
+            packed.at[k, peer_plane],
+            arrived.at[k, mine],
+            out_sem.at[k, peer_plane],
+            in_sem.at[k, mine],
+            peer_plane * group + lane,
+        )
+
+    def from_plane(k, step):
+        source = lax.rem(mine + EXPERTS - step, EXPERTS)
+        return push(
+            packed.at[k, source],
+            arrived.at[k, source],
+            out_sem.at[k, source],
+            in_sem.at[k, source],
+            source * group + lane,
+        )
+
+    for k in range(chunk_count):
+        cols = slice(k * width, (k + 1) * width)
+        normal = (hidden[:, cols] * level * gain[:, cols].astype(f32)).astype(bf16)
+        normed[:, cols] = normal
+        spread = jnp.dot(placing, normal, preferred_element_type=f32)
+        for e in range(EXPERTS):
+            packed[k, e] = spread[e * padded : e * padded + CAP].astype(bf16)
+        for step in range(1, EXPERTS):
+            to_plane(k, step).start()
+        arrived[k, mine] = packed[k, mine]
+
+    embed_row[...] = embed[...].astype(f32)
+
+    def block_push(source, j):
+        target = blocks.at[me]
+        return push(source, target, block_out_sem.at[j], block_in_sem.at[me], j)
+
+    def send_block(row, b, j):
+        source = row.at[:, b * depth : (b + 1) * depth]
+
+        @pl.when(me != j)
+        def _():
+            block_push(source, j).start()
+
+        @pl.when(me == j)
+        def _():
+            blocks[j] = row[:, b * depth : (b + 1) * depth]
+
+    def wait_block(row, b, j):
+        @pl.when(me != j)
+        def _():
+            block_push(row.at[:, b * depth : (b + 1) * depth], j).wait_send()
+
+    for b in range(block_count):
+        send_block(embed_row, b, block_count + b)
+
+    logits = [jnp.zeros((padded, 1), f32) for _ in range(EXPERTS)]
+    for k in range(chunk_count):
+        cols = slice(k * width, (k + 1) * width)
+        normal = normed[:, cols].astype(f32)
+        for e in range(EXPERTS):
+            logits[e] = logits[e] + jnp.sum(
+                normal * router[e : e + 1, cols].astype(f32), axis=-1, keepdims=True
+            )
+    ids = [jnp.full((padded, 1), -1, jnp.int32) for _ in range(4)]
+    token_row = row8[:, 0:1]
+    for token, choices in enumerate(places):
+        for choice, (expert, rank) in enumerate(choices):
+            ids[choice] = jnp.where(token_row == token, expert, ids[choice])
+            ids[2 + choice] = jnp.where(token_row == token, expert * CAP + rank, ids[2 + choice])
+    first_logit = jnp.zeros((padded, 1), f32)
+    second_logit = jnp.zeros((padded, 1), f32)
+    for e in range(EXPERTS):
+        first_logit = first_logit + jnp.where(ids[0] == e, logits[e], 0.0)
+        second_logit = second_logit + jnp.where(ids[1] == e, logits[e], 0.0)
+    first_share = jax.nn.sigmoid(first_logit - second_logit)
+    share_col = col8[:, :share]
+    weighted = jnp.where(share_col == ids[2], first_share, 0.0) + jnp.where(
+        share_col == ids[3], 1.0 - first_share, 0.0
+    )
+    high = weighted.astype(bf16)
+    middle = (weighted - high.astype(f32)).astype(bf16)
+    low = (weighted - high.astype(f32) - middle.astype(f32)).astype(bf16)
+    mixers = jnp.concatenate(
+        [high.astype(f32), middle.astype(f32), low.astype(f32)], axis=0
+    ).astype(bf16)
+
+    own_rows = pl.ds(pl.multiple_of(lane * share, share), share)
+
+    def in_plane(k, step):
+        peer = mine * group + lax.rem(lane + step, group)
+        return push(
+            rows.at[k, own_rows, :],
+            rows.at[k, own_rows, :],
+            plane_out_sem.at[k, step],
+            plane_in_sem.at[k, step],
+            peer,
+        )
+
+    def out_of_plane(k, step):
+        source = lax.rem(lane + group - step, group)
+        block = rows.at[k, pl.ds(pl.multiple_of(source * share, share), share), :]
+        return push(
+            block,
+            block,
+            plane_out_sem.at[k, step],
+            plane_in_sem.at[k, step],
+            mine * group + source,
+        )
+
+    for k in range(chunk_count):
+        for step in range(1, EXPERTS):
+            from_plane(k, step).wait_recv()
+        rows[k, own_rows, :] = jnp.concatenate(
+            [arrived[k, s].astype(f32) for s in range(EXPERTS)], axis=0
+        ).astype(bf16)
+        for step in range(1, group):
+            in_plane(k, step).start()
+
+    for k in range(chunk_count):
+        for step in range(1, group):
+            out_of_plane(k, step).wait_recv()
+        for h in range(half_count):
+            cols = slice(h * SLICE, (h + 1) * SLICE)
+            sums = []
+            for i, total in ((2 * (k * half_count + h), gate_sum), (2 * (k * half_count + h) + 1, up_sum)):
+                for copy in load_copies(i):
+                    copy.wait()
+                value = jnp.dot(rows[k], weights[i % slots], preferred_element_type=f32)
+                if k > 0:
+                    value = value + total[:, cols]
+                if k < chunk_count - 1:
+                    total[:, cols] = value
+                sums.append(value)
+                start_load(i + slots)
+            if k == chunk_count - 1:
+                activation[:, cols] = (jax.nn.silu(sums[0]) * sums[1]).astype(bf16)
+
+    def to_owner_lane(p, step):
+        peer = lax.rem(lane + step, group)
+        return push(
+            leaving.at[p, peer],
+            returned.at[p, lane],
+            back_out_sem.at[p, peer],
+            back_in_sem.at[p, lane],
+            mine * group + peer,
+        )
+
+    def from_member(p, step):
+        source = lax.rem(lane + group - step, group)
+        return push(
+            leaving.at[p, source],
+            returned.at[p, source],
+            back_out_sem.at[p, source],
+            back_in_sem.at[p, source],
+            mine * group + source,
+        )
+
+    def to_home(p, step):
+        plane = lax.rem(mine + step, EXPERTS)
+        return push(
+            home_leaving.at[p, plane],
+            home_returned.at[p, mine],
+            home_out_sem.at[p, plane],
+            home_in_sem.at[p, mine],
+            plane * group + lane,
+        )
+
+    def from_expert(p, step):
+        plane = lax.rem(mine + EXPERTS - step, EXPERTS)
+        return push(
+            home_leaving.at[p, plane],
+            home_returned.at[p, plane],
+            home_out_sem.at[p, plane],
+            home_in_sem.at[p, plane],
+            plane * group + lane,
+        )
+
+    def partial_step(p):
+        i = pair_loads + p
+        for copy in load_copies(i):
+            copy.wait()
+        partial = jnp.dot(activation[...], weights[i % slots], preferred_element_type=f32)
+        start_load(i + slots)
+        for member in range(group):
+            leaving[p, member] = partial[member * share : (member + 1) * share].astype(bf16)
+        for step in range(1, group):
+            to_owner_lane(p, step).start()
+        returned[p, lane] = leaving[p, lane]
+
+    def plane_step(p):
+        for step in range(1, group):
+            from_member(p, step).wait_recv()
+        total = returned[p, 0].astype(f32)
+        for member in range(1, group):
+            total = total + returned[p, member].astype(f32)
+        for s in range(EXPERTS):
+            home_leaving[p, s] = total[s * CAP : (s + 1) * CAP].astype(bf16)
+        for step in range(1, EXPERTS):
+            to_home(p, step).start()
+        home_returned[p, mine] = home_leaving[p, mine]
+
+    sent = [0]
+
+    def home_step(p):
+        for step in range(1, EXPERTS):
+            from_expert(p, step).wait_recv()
+        cols = slice(p * SLICE, (p + 1) * SLICE)
+        block = jnp.concatenate(
+            [home_returned[p, e].astype(f32) for e in range(EXPERTS)], axis=0
+        ).astype(bf16)
+        mixed = jnp.dot(mixers, block, preferred_element_type=f32)
+        expert_sum = mixed[:padded] + mixed[padded : 2 * padded] + mixed[2 * padded :]
+        result = (hidden[:, cols] + expert_sum).astype(bf16)
+        layer_out[:, cols] = result[:TREE_NODES]
+        picked[:, cols] = jnp.sum(
+            jnp.where(token_row == accepted[0], result.astype(f32), 0.0), axis=0, keepdims=True
+        )
+        while sent[0] < block_count and (sent[0] + 1) * depth <= (p + 1) * SLICE:
+            send_block(picked, sent[0], sent[0])
+            sent[0] += 1
+
+    lag_plane, lag_home = 1, 3
+    for p in range(piece_count + lag_home):
+        if p < piece_count:
+            partial_step(p)
+        if 0 <= p - lag_plane < piece_count:
+            plane_step(p - lag_plane)
+        if 0 <= p - lag_home < piece_count:
+            home_step(p - lag_home)
+
+    def take(k, carry):
+        source = lax.rem(me + n - k, n)
+        push(
+            blocks.at[source], blocks.at[source], block_out_sem.at[source], block_in_sem.at[source], source
+        ).wait_recv()
+        block_rows[pl.ds(source, 1), :] = blocks[source]
+        return carry
+
+    block_rows[pl.ds(me, 1), :] = blocks[me]
+    lax.fori_loop(1, n, take, 0)
+    draft_rows = block_rows[...].astype(bf16)
+    for p in range(piece_count):
+        i = down_loads + p // stacked
+        fc_copy(p).wait()
+        first = p % stacked * depth
+        partial = jnp.dot(
+            draft_rows, weights[i % slots, first : first + depth, :], preferred_element_type=f32
+        )
+        for source in range(n):
+            line = partial[source : source + 1]
+            draft_leaving[source, p] = jnp.concatenate(
+                [line[:, :half], line[:, half:]], axis=0
+            ).astype(bf16)
+
+    def send_partial(k, carry):
+        peer = lax.rem(me + k, n)
+        push(
+            draft_leaving.at[peer],
+            draft_returned.at[me],
+            draft_out_sem.at[peer],
+            draft_in_sem.at[me],
+            peer,
+        ).start()
+        return carry
+
+    lax.fori_loop(1, n, send_partial, 0)
+    draft_returned[me] = draft_leaving[me]
+
+    def drain(k, carry):
+        peer = lax.rem(me + n - k, n)
+        push(
+            draft_leaving.at[peer],
+            draft_returned.at[peer],
+            draft_out_sem.at[peer],
+            draft_in_sem.at[peer],
+            peer,
+        ).wait()
+        return carry
+
+    lax.fori_loop(1, n, drain, 0)
+    for p in range(piece_count):
+        total = draft_returned[0, p].astype(f32)
+        for source in range(1, n):
+            total = total + draft_returned[source, p].astype(f32)
+        start = p * SLICE
+        draft_out[:, start : start + half] = total[0:1].astype(bf16)
+        draft_out[:, start + half : start + SLICE] = total[1:2].astype(bf16)
+
+    for k in range(chunk_count):
+        for step in range(1, EXPERTS):
+            from_plane(k, step).wait_send()
+        for step in range(1, group):
+            in_plane(k, step).wait_send()
+    for p in range(piece_count):
+        for step in range(1, group):
+            from_member(p, step).wait_send()
+        for step in range(1, EXPERTS):
+            from_expert(p, step).wait_send()
+    for b in range(block_count):
+        wait_block(picked, b, b)
+        wait_block(embed_row, b, block_count + b)
+
+
+def fused(
+    queries,
+    tree_key_value,
+    key_value_cache,
+    lengths,
+    parents,
+    residual,
+    ffn_gain,
+    router,
+    routes,
+    gate_weight,
+    up_weight,
+    down_weight,
+    accepted,
+    next_embed,
+    draft_fc,
+    n,
+):
+    width, model_width = down_weight.shape
+    depth = draft_fc.shape[0]
+    group = n // EXPERTS
+    share = EXPERTS * CAP
+    slots = 13
+    chunks = model_width // width
+    pieces = model_width // SLICE
+    stacked = width // depth
+    loads = 2 * chunks * (width // SLICE) + pieces + -(-pieces // stacked)
+    kv_width = tree_key_value.shape[2]
+    key_rows = key_value_cache.shape[2] + 128
+    anywhere = pl.BlockSpec(memory_space=pl.ANY)
+    scalars = pl.BlockSpec(memory_space=pltpu.SMEM)
+    whole = pl.BlockSpec(memory_space=pltpu.VMEM)
+    bf16, f32 = jnp.bfloat16, jnp.float32
+    dma = pltpu.SemaphoreType.DMA
+    return pl.pallas_call(
+        functools.partial(fused_kernel, n, slots),
+        out_shape=(
+            jax.ShapeDtypeStruct((TREE_NODES, model_width), bf16),
+            jax.ShapeDtypeStruct((1, model_width), bf16),
+        ),
+        in_specs=[scalars] * 4 + [anywhere] * 11,
+        out_specs=(whole, whole),
+        scratch_shapes=[
+            pltpu.VMEM((slots, width, SLICE), bf16),
+            pltpu.VMEM((TREE_NODES, model_width), bf16),
+            pltpu.VMEM((TREE_NODES, 2, kv_width), bf16),
+            pltpu.VMEM((key_rows, kv_width), bf16),
+            pltpu.VMEM((key_rows, kv_width), bf16),
+            pltpu.VMEM((TREE_NODES, model_width), bf16),
+            pltpu.VMEM((1, model_width), bf16),
+            pltpu.VMEM((EXPERTS, model_width), bf16),
+            pltpu.VMEM((1, model_width), bf16),
+            pltpu.VMEM((2, 16, kv_width), f32),
+            pltpu.VMEM((8, model_width), f32),
+            pltpu.VMEM((8, model_width), bf16),
+            pltpu.VMEM((chunks, EXPERTS, CAP, width), bf16),
+            pltpu.VMEM((chunks, EXPERTS, CAP, width), bf16),
+            pltpu.VMEM((chunks, group * share, width), bf16),
+            pltpu.VMEM((group * share, width), f32),
+            pltpu.VMEM((group * share, width), f32),
+            pltpu.VMEM((group * share, width), bf16),
+            pltpu.VMEM((pieces, group, share, SLICE), bf16),
+            pltpu.VMEM((pieces, group, share, SLICE), bf16),
+            pltpu.VMEM((pieces, EXPERTS, CAP, SLICE), bf16),
+            pltpu.VMEM((pieces, EXPERTS, CAP, SLICE), bf16),
+            pltpu.VMEM((1, model_width), f32),
+            pltpu.VMEM((1, model_width), f32),
+            pltpu.VMEM((n, 1, depth), f32),
+            pltpu.VMEM((n, depth), f32),
+            pltpu.VMEM((n, pieces, 2, SLICE // 2), bf16),
+            pltpu.VMEM((n, pieces, 2, SLICE // 2), bf16),
+            dma((loads, stacked)),
+            dma((8,)),
+            dma((chunks, EXPERTS)),
+            dma((chunks, EXPERTS)),
+            dma((chunks, group)),
+            dma((chunks, group)),
+            dma((pieces, group)),
+            dma((pieces, group)),
+            dma((pieces, EXPERTS)),
+            dma((pieces, EXPERTS)),
+            dma((n,)),
+            dma((n,)),
+            dma((n,)),
+            dma((n,)),
+        ],
+        compiler_params=pltpu.CompilerParams(
+            collective_id=0, has_side_effects=True, vmem_limit_bytes=67_000_000
+        ),
+        name="fused",
+    )(
+        lengths,
+        parents,
+        routes.T,
+        accepted,
+        queries,
+        tree_key_value,
+        key_value_cache,
+        residual,
+        ffn_gain.reshape(1, model_width),
+        router.T,
+        next_embed,
+        gate_weight,
+        up_weight,
+        down_weight,
+        draft_fc,
+    )
+
+
+def fits(lengths, gate_weight, draft_fc, n):
+    model_width, width = gate_weight.shape
+    depth = draft_fc.shape[0]
+    return (
+        lengths.shape[0] == 1
+        and n % EXPERTS == 0
+        and width % SLICE == 0
+        and model_width % width == 0
+        and model_width % SLICE == 0
+        and depth % 128 == 0
+        and width % depth <= width // 2
+        and depth <= width
+        and n * depth == 2 * model_width
+        and n * CAP <= 128
+    )
+
+
 def per_device(
     queries,
     tree_key_value,
@@ -486,6 +1177,25 @@
     draft_fc,
 ):
     devices = lax.axis_size("expert")
+    if fits(lengths, gate_weight, draft_fc, devices):
+        return fused(
+            queries,
+            tree_key_value,
+            key_value_cache,
+            lengths,
+            parents,
+            residual,
+            ffn_gain,
+            router,
+            routes,
+            gate_weight,
+            up_weight,
+            down_weight,
+            accepted,
+            next_embed,
+            draft_fc,
+            devices,
+        )
     context = attention(queries, tree_key_value, key_value_cache, lengths, parents)
     hidden_state = residual.astype(jnp.float32) + context
     normed = (

time: 91.4 us -> 75.1 us (0.82)
  other arithmetic: 6.17 us -> 0 us
  matrix products: 4.79 us -> 0 us
  Pallas kernels: 72 us -> 68.7 us
  local copies, waits for them, and re-layouts: 5.61 us -> 4.24 us
    dot_general x8 -> x0, matrix products: 4.79 us -> none  [the longest x1 1.88 us: per_device(): jnp.einsum('ect,ecd->td', weighted, grouped, precision=lax.Precision.HIGH...]
    convert_element_type x6 -> x0, other arithmetic: 3.74 us -> none  [the longest x2 2.03 us: per_device(): draft_out = draft(blocks.astype(jnp.float32), draft_fc).astype(jnp.bfloat16)]
    pallas_call x3 -> x1, Pallas kernels: 72 us -> 68.7 us  [fused(): pl.pallas_call(functools.partial(fused_kernel, n, slots), out_shape=(jax....]
    slice x2 -> x0, local copies, waits for them, and re-layouts: 2.66 us -> none  [the longest x1 1.72 us: attention(): key_value_cache[:, 1]]
    unnamed x12 -> x2, local copies, waits for them, and re-layouts: 1.12 us -> 2.91 us
    reduce_sum x3 -> x0, other arithmetic: 1.45 us -> none  [the longest x1 1.07 us: per_device(): jnp.mean(hidden_state * hidden_state, axis=-1, keepdims=True) + EPSILON]
    reshape x1, local copies, waits for them, and re-layouts: 0.04 us -> 1.33 us  [fused(): ffn_gain.reshape(1, model_width)]
    another operation x1 -> x0, local copies, waits for them, and re-layouts: 1 us -> none
where the time goes in v1:
time: 75.1 us; the launch traced here: 74.8 us
  Pallas kernels  68.7 us (91%)
  local copies, waits for them, and re-layouts  4.24 us (6%)
  between operations  1.93 us (3%)
    pallas_call x1, Pallas kernels, fused(): pl.pallas_call(functools.partial(fused_kernel, n, slots), out_shape=(jax....  68.7 us
    unnamed x2, local copies, waits for them, and re-layouts  2.91 us

profile of v1, /device:TPU:0, one launch (start us, length us, event | category | flops | bytes accessed | tf_op | source)
XLA Modules:
  0.0 74.8 jit_solution(10312877689869727831)
XLA Ops:
  1.9 1.3 %reshape.7.gain_hbm = bf16[1,6144]{1,0:T(2,128)(2,1)} reshape(bf16[6144]{0:T(1024)(128)(2,1)} %param.21) | data formatting | bytes 24576 | tf_op jit(solution)/shard_map/reshape | solution.py:1135
  3.3 68.7 %fused.1 = (bf16[6,6144]{1,0:T(8,128)(2,1)}, bf16[1,6144]{1,0:T(2,128)(2,1)}) custom-call(s32[1]{0:T(128)S(6)} %copy.19.lengths, s32[6]{0:T(128)} %parents.1, s32[2,6]{1,0:T(2,128)} %bitcast.3, s32[1]{0:T(128)S(6)} %copy.20.accepted, bf16[6,6144]{1,0:T(8,128)(2,1)} %queries_hbm.1, bf16[6,2,1024]{2,1,0:T(2,128)(2,1)} %tree_hbm.1, ...), custom_call_target="tpu_custom_call" | custom-call | tf_op jit(solution)/shard_map/fused/pallas_call | solution.py:1070
  71.9 1.5 %copy.21 = bf16[6,6144]{1,0:T(8,128)(2,1)} copy(bf16[6,6144]{1,0:T(8,128)(2,1)} %get-tuple-element.4) | data formatting | bytes 147456
  73.5 1.4 %copy.22 = bf16[1,6144]{1,0:T(2,128)(2,1)} copy(bf16[1,6144]{1,0:T(2,128)(2,1)} %get-tuple-element.5) | data formatting | bytes 24576

commit v2 on v1

--- a/solution.py
+++ b/solution.py
@@ -469,6 +469,7 @@
 
 
 SLICE = 1024
+LANES = 128
 
 
 def greet_all(n, me):
@@ -520,14 +521,19 @@
     gate_sum,
     up_sum,
     activation,
+    kept,
     leaving,
     returned,
+    chip_sum,
+    chip_leaving,
+    chip_returned,
     home_leaving,
     home_returned,
     picked,
     embed_row,
     blocks,
     block_rows,
+    draft_wide,
     draft_leaving,
     draft_returned,
     load_sem,
@@ -536,8 +542,10 @@
     in_sem,
     plane_out_sem,
     plane_in_sem,
-    back_out_sem,
-    back_in_sem,
+    core_out_sem,
+    core_in_sem,
+    chip_out_sem,
+    chip_in_sem,
     home_out_sem,
     home_in_sem,
     block_out_sem,
@@ -550,49 +558,53 @@
     group = n // EXPERTS
     mine = me // group
     lane = lax.rem(me, group)
+    core = lax.rem(lane, 2)
+    across = lane // 2
+    core_peer = mine * group + across * 2 + (1 - core)
+    chip_peer = mine * group + (1 - across) * 2 + core
     model_width = down_hbm.shape[1]
     width = down_hbm.shape[0]
     depth = fc_hbm.shape[0]
-    chunk_count = model_width // width
+    chunk_count = model_width // SLICE
     half_count = width // SLICE
     piece_count = model_width // SLICE
-    stacked = width // depth
-    pair_loads = 2 * chunk_count * half_count
-    down_loads = pair_loads + piece_count
-    load_count = down_loads + -(-piece_count // stacked)
     block_count = model_width // depth
-    half = SLICE // 2
     padded = 8
     share = EXPERTS * CAP
     cache_slots = cache_hbm.shape[2]
     key_rows = keys.shape[0]
-
-    def fc_copy(p):
-        i, part = down_loads + p // stacked, p % stacked
-        return pltpu.make_async_copy(
-            fc_hbm.at[:, p * SLICE : (p + 1) * SLICE],
-            weights.at[i % slots, part * depth : (part + 1) * depth, :],
-            load_sem.at[i, part],
-        )
-
-    def load_copies(i):
+    line_count = model_width // LANES
+    lines = SLICE // LANES
+    part_count = draft_leaving.shape[0]
+
+    pairs = [
+        ("pair", k, h, i) for k in range(chunk_count) for h in range(half_count) for i in range(2)
+    ]
+    downs = [("down", p, a) for p in range(piece_count) for a in range(half_count)]
+    fcs = [("fc", p) for p in range(piece_count)]
+    early = len(downs) // 2
+    order = pairs + downs[:early] + fcs + downs[early:]
+    place = {item: i for i, item in enumerate(order)}
+
+    def load_copy(item):
+        i = place[item]
         slot = weights.at[i % slots]
-        if i < pair_loads:
-            source = gate_hbm if i % 2 == 0 else up_hbm
-            k, h = i // (2 * half_count), i // 2 % half_count
-            view = source.at[k * width : (k + 1) * width, h * SLICE : (h + 1) * SLICE]
-            return [pltpu.make_async_copy(view, slot, load_sem.at[i, 0])]
-        if i < down_loads:
-            p = i - pair_loads
-            view = down_hbm.at[:, p * SLICE : (p + 1) * SLICE]
-            return [pltpu.make_async_copy(view, slot, load_sem.at[i, 0])]
-        first = (i - down_loads) * stacked
-        return [fc_copy(p) for p in range(first, min(first + stacked, piece_count))]
+        if item[0] == "pair":
+            k, h = item[1], item[2]
+            source = (gate_hbm, up_hbm)[item[3]]
+            view = source.at[k * SLICE : (k + 1) * SLICE, h * SLICE : (h + 1) * SLICE]
+        elif item[0] == "down":
+            p, a = item[1], item[2]
+            view = down_hbm.at[a * SLICE : (a + 1) * SLICE, p * SLICE : (p + 1) * SLICE]
+        else:
+            p = item[1]
+            view = fc_hbm.at[:, p * SLICE : (p + 1) * SLICE]
+            slot = weights.at[i % slots, 0:depth, :]
+        return pltpu.make_async_copy(view, slot, load_sem.at[i])
 
     def start_load(i):
-        if i < load_count:
-            for copy in load_copies(i):
-                copy.start()
+        if i < len(order):
+            load_copy(order[i]).start()
 
     inputs = [
         pltpu.make_async_copy(source, target, input_sem.at[i])
@@ -611,15 +623,13 @@
     ]
     for copy in inputs:
         copy.start()
-    for i in range(slots):
-        start_load(i)
     barrier = greet_all(n, me)
 
-    row8 = lax.broadcasted_iota(jnp.int32, (padded, 128), 0)
-    col8 = lax.broadcasted_iota(jnp.int32, (padded, 128), 1)
-    node_ids = lax.broadcasted_iota(jnp.int32, (1, 128), 1)
+    row8 = lax.broadcasted_iota(jnp.int32, (padded, LANES), 0)
+    col8 = lax.broadcasted_iota(jnp.int32, (padded, LANES), 1)
+    node_ids = lax.broadcasted_iota(jnp.int32, (1, LANES), 1)
     reached = []
-    related = jnp.zeros((padded, 128), f32)
+    related = jnp.zeros((padded, LANES), f32)
     for node in range(TREE_NODES):
         row = (node_ids == node).astype(f32)
         parent = parents[node]
@@ -650,18 +660,19 @@
 
     for copy in inputs[:3]:
         copy.wait()
+    for i in range(slots):
+        start_load(i)
     tree_rows[...] = jnp.zeros_like(tree_rows)
     for token in range(TREE_NODES):
         both = tree[token].astype(f32)
         tree_rows[0, token : token + 1, :] = both[0:1]
         tree_rows[1, token : token + 1, :] = both[1:2]
     tile = tree_rows.shape[1]
+    blank = jnp.zeros((key_rows - cache_slots - tile, keys.shape[1]), bf16)
     keys[cache_slots : cache_slots + tile, :] = tree_rows[0].astype(bf16)
-    keys[cache_slots + tile :, :] = jnp.zeros((key_rows - cache_slots - tile, keys.shape[1]), bf16)
+    keys[cache_slots + tile :, :] = blank
     values[cache_slots : cache_slots + tile, :] = tree_rows[1].astype(bf16)
-    values[cache_slots + tile :, :] = jnp.zeros(
-        (key_rows - cache_slots - tile, keys.shape[1]), bf16
-    )
+    values[cache_slots + tile :, :] = blank
     spare = jnp.zeros((padded - TREE_NODES, HEAD_SIZE), f32)
     score_scale = HEAD_SIZE ** (-0.5)
     weights_of = []
@@ -719,39 +730,30 @@
 
     pl.semaphore_wait(barrier, n - 1)
 
-    def push(src, dst, send_sem, recv_sem, peer):
-        return pltpu.make_async_remote_copy(
-            src_ref=src,
-            dst_ref=dst,
-            send_sem=send_sem,
-            recv_sem=recv_sem,
-            device_id={"expert": peer},
-            device_id_type=pl.DeviceIdType.MESH,
-        )
-
     def to_plane(k, step):
-        peer_plane = lax.rem(mine + step, EXPERTS)
+        plane = lax.rem(mine + step, EXPERTS)
         return push(
-            packed.at[k, peer_plane],
+            packed.at[k, plane],
             arrived.at[k, mine],
-            out_sem.at[k, peer_plane],
+            out_sem.at[k, plane],
             in_sem.at[k, mine],
-            peer_plane * group + lane,
+            plane * group + lane,
         )
 
     def from_plane(k, step):
-        source = lax.rem(mine + EXPERTS - step, EXPERTS)
+        plane = lax.rem(mine + EXPERTS - step, EXPERTS)
         return push(
-            packed.at[k, source],
-            arrived.at[k, source],
-            out_sem.at[k, source],
-            in_sem.at[k, source],
-            source * group + lane,
+            packed.at[k, plane],
+            arrived.at[k, plane],
+            out_sem.at[k, plane],
+            in_sem.at[k, plane],
+            plane * group + lane,
         )
 
     for k in range(chunk_count):
-        cols = slice(k * width, (k + 1) * width)
-        normal = (hidden[:, cols] * level * gain[:, cols].astype(f32)).astype(bf16)
+        cols = slice(k * SLICE, (k + 1) * SLICE)
+        gains = [gain[k * lines + t : k * lines + t + 1, :].astype(f32) for t in range(lines)]
+        normal = (hidden[:, cols] * level * jnp.concatenate(gains, axis=1)).astype(bf16)
         normed[:, cols] = normal
         spread = jnp.dot(placing, normal, preferred_element_type=f32)
         for e in range(EXPERTS):
@@ -762,16 +764,14 @@
 
     embed_row[...] = embed[...].astype(f32)
 
-    def block_push(source, j):
-        target = blocks.at[me]
-        return push(source, target, block_out_sem.at[j], block_in_sem.at[me], j)
+    def block_push(row, b, j):
+        source = row.at[:, b * depth : (b + 1) * depth]
+        return push(source, blocks.at[me], block_out_sem.at[j], block_in_sem.at[me], j)
 
     def send_block(row, b, j):
-        source = row.at[:, b * depth : (b + 1) * depth]
-
         @pl.when(me != j)
         def _():
-            block_push(source, j).start()
+            block_push(row, b, j).start()
 
         @pl.when(me == j)
         def _():
@@ -780,14 +780,14 @@
     def wait_block(row, b, j):
         @pl.when(me != j)
         def _():
-            block_push(row.at[:, b * depth : (b + 1) * depth], j).wait_send()
+            block_push(row, b, j).wait_send()
 
     for b in range(block_count):
         send_block(embed_row, b, block_count + b)
 
     logits = [jnp.zeros((padded, 1), f32) for _ in range(EXPERTS)]
     for k in range(chunk_count):
-        cols = slice(k * width, (k + 1) * width)
+        cols = slice(k * SLICE, (k + 1) * SLICE)
         normal = normed[:, cols].astype(f32)
         for e in range(EXPERTS):
             logits[e] = logits[e] + jnp.sum(
@@ -809,82 +809,76 @@
     weighted = jnp.where(share_col == ids[2], first_share, 0.0) + jnp.where(
         share_col == ids[3], 1.0 - first_share, 0.0
     )
-    high = weighted.astype(bf16)
-    middle = (weighted - high.astype(f32)).astype(bf16)
-    low = (weighted - high.astype(f32) - middle.astype(f32)).astype(bf16)
-    mixers = jnp.concatenate(
-        [high.astype(f32), middle.astype(f32), low.astype(f32)], axis=0
-    ).astype(bf16)
-
-    own_rows = pl.ds(pl.multiple_of(lane * share, share), share)
-
-    def in_plane(k, step):
-        peer = mine * group + lax.rem(lane + step, group)
-        return push(
-            rows.at[k, own_rows, :],
-            rows.at[k, own_rows, :],
-            plane_out_sem.at[k, step],
-            plane_in_sem.at[k, step],
-            peer,
-        )
-
-    def out_of_plane(k, step):
-        source = lax.rem(lane + group - step, group)
-        block = rows.at[k, pl.ds(pl.multiple_of(source * share, share), share), :]
-        return push(
-            block,
-            block,
-            plane_out_sem.at[k, step],
-            plane_in_sem.at[k, step],
-            mine * group + source,
-        )
-
-    for k in range(chunk_count):
+    high = weighted.astype(bf16).astype(f32)
+    middle = (weighted - high).astype(bf16).astype(f32)
+    low = weighted - high - middle
+    mixers = jnp.concatenate([high, middle, low], axis=0).astype(bf16)
+
+    def lane_rows(k, which):
+        return rows.at[k, pl.ds(pl.multiple_of(which * share, share), share), :]
+
+    def row_push(k, which, sem, peer):
+        block = lane_rows(k, which)
+        return push(block, block, plane_out_sem.at[k, sem], plane_in_sem.at[k, sem], peer)
+
+    chip_lane = (1 - across) * 2 + core
+    core_lane = across * 2 + (1 - core)
+    far_lane = (1 - across) * 2 + (1 - core)
+
+    def gather_step(k):
         for step in range(1, EXPERTS):
             from_plane(k, step).wait_recv()
-        rows[k, own_rows, :] = jnp.concatenate(
+        rows[k, pl.ds(pl.multiple_of(lane * share, share), share), :] = jnp.concatenate(
             [arrived[k, s].astype(f32) for s in range(EXPERTS)], axis=0
         ).astype(bf16)
-        for step in range(1, group):
-            in_plane(k, step).start()
-
-    for k in range(chunk_count):
-        for step in range(1, group):
-            out_of_plane(k, step).wait_recv()
+        row_push(k, lane, 0, chip_peer).start()
+        row_push(k, lane, 1, core_peer).start()
+
+    def forward_step(k):
+        row_push(k, chip_lane, 0, chip_peer).wait_recv()
+        row_push(k, chip_lane, 2, core_peer).start()
+
+    def expert_step(k):
+        row_push(k, core_lane, 1, core_peer).wait_recv()
+        row_push(k, far_lane, 2, core_peer).wait_recv()
         for h in range(half_count):
             cols = slice(h * SLICE, (h + 1) * SLICE)
             sums = []
-            for i, total in ((2 * (k * half_count + h), gate_sum), (2 * (k * half_count + h) + 1, up_sum)):
-                for copy in load_copies(i):
-                    copy.wait()
-                value = jnp.dot(rows[k], weights[i % slots], preferred_element_type=f32)
+            for i, total in ((0, gate_sum), (1, up_sum)):
+                item = ("pair", k, h, i)
+                load_copy(item).wait()
+                value = jnp.dot(
+                    rows[k], weights[place[item] % slots], preferred_element_type=f32
+                )
                 if k > 0:
                     value = value + total[:, cols]
                 if k < chunk_count - 1:
                     total[:, cols] = value
                 sums.append(value)
-                start_load(i + slots)
+                start_load(place[item] + slots)
             if k == chunk_count - 1:
-                activation[:, cols] = (jax.nn.silu(sums[0]) * sums[1]).astype(bf16)
-
-    def to_owner_lane(p, step):
-        peer = lax.rem(lane + step, group)
+                activation[h] = (jax.nn.silu(sums[0]) * sums[1]).astype(bf16)
+
+    for t in range(chunk_count + 6):
+        if t < chunk_count:
+            gather_step(t)
+        if 0 <= t - 2 < chunk_count:
+            forward_step(t - 2)
+        if 0 <= t - 3 < chunk_count:
+            expert_step(t - 3)
+
+    def core_push(p):
         return push(
-            leaving.at[p, peer],
-            returned.at[p, lane],
-            back_out_sem.at[p, peer],
-            back_in_sem.at[p, lane],
-            mine * group + peer,
-        )
-
-    def from_member(p, step):
-        source = lax.rem(lane + group - step, group)
+            leaving.at[p], returned.at[p], core_out_sem.at[p], core_in_sem.at[p], core_peer
+        )
+
+    def chip_push(p):
         return push(
-            leaving.at[p, source],
-            returned.at[p, source],
-            back_out_sem.at[p, source],
-            back_in_sem.at[p, source],
-            mine * group + source,
+            chip_leaving.at[p],
+            chip_returned.at[p],
+            chip_out_sem.at[p],
+            chip_in_sem.at[p],
+            chip_peer,
         )
 
     def to_home(p, step):
@@ -908,23 +902,39 @@
         )
 
     def partial_step(p):
-        i = pair_loads + p
-        for copy in load_copies(i):
-            copy.wait()
-        partial = jnp.dot(activation[...], weights[i % slots], preferred_element_type=f32)
-        start_load(i + slots)
+        partial = None
+        for a in range(half_count):
+            item = ("down", p, a)
+            load_copy(item).wait()
+            value = jnp.dot(
+                activation[a], weights[place[item] % slots], preferred_element_type=f32
+            )
+            partial = value if partial is None else partial + value
+            start_load(place[item] + slots)
         for member in range(group):
-            leaving[p, member] = partial[member * share : (member + 1) * share].astype(bf16)
-        for step in range(1, group):
-            to_owner_lane(p, step).start()
-        returned[p, lane] = leaving[p, lane]
-
-    def plane_step(p):
-        for step in range(1, group):
-            from_member(p, step).wait_recv()
-        total = returned[p, 0].astype(f32)
-        for member in range(1, group):
-            total = total + returned[p, member].astype(f32)
+            block = partial[member * share : (member + 1) * share].astype(bf16)
+            a, c = member // 2, member % 2
+
+            @pl.when(core == c)
+            def _():
+                kept[p, a] = block
+
+            @pl.when(core != c)
+            def _():
+                leaving[p, a] = block
+
+        core_push(p).start()
+
+    def core_step(p):
+        core_push(p).wait_recv()
+        far = 1 - across
+        chip_leaving[p] = (kept[p, far].astype(f32) + returned[p, far].astype(f32)).astype(bf16)
+        chip_push(p).start()
+        chip_sum[p] = kept[p, across].astype(f32) + returned[p, across].astype(f32)
+
+    def chip_step(p):
+        chip_push(p).wait_recv()
+        total = chip_sum[p] + chip_returned[p].astype(f32)
         for s in range(EXPERTS):
             home_leaving[p, s] = total[s * CAP : (s + 1) * CAP].astype(bf16)
         for step in range(1, EXPERTS):
@@ -951,86 +961,112 @@
             send_block(picked, sent[0], sent[0])
             sent[0] += 1
 
-    lag_plane, lag_home = 1, 3
-    for p in range(piece_count + lag_home):
+    def draft_push(q, peer, at):
+        return push(
+            draft_leaving.at[q, peer],
+            draft_returned.at[q, at],
+            draft_out_sem.at[q, peer],
+            draft_in_sem.at[q, at],
+            peer,
+        )
+
+    def draft_step():
+        def take(k, carry):
+            source = lax.rem(me + n - k, n)
+            push(
+                blocks.at[source],
+                blocks.at[source],
+                block_out_sem.at[source],
+                block_in_sem.at[source],
+                source,
+            ).wait_recv()
+            block_rows[pl.ds(source, 1), :] = blocks[source]
+            return carry
+
+        block_rows[pl.ds(me, 1), :] = blocks[me]
+        lax.fori_loop(1, n, take, 0)
+        draft_rows = block_rows[...].astype(bf16)
+        for q in range(part_count):
+            for p in range(q * piece_count // part_count, (q + 1) * piece_count // part_count):
+                item = ("fc", p)
+                load_copy(item).wait()
+                partial = jnp.dot(
+                    draft_rows, weights[place[item] % slots, 0:depth, :], preferred_element_type=f32
+                )
+                for t in range(lines):
+                    draft_wide[pl.ds(p * lines + t, n, stride=line_count), :] = partial[
+                        :, t * LANES : (t + 1) * LANES
+                    ]
+            each = line_count // part_count
+            for source in range(n):
+                start = source * line_count + q * each
+                draft_leaving[q, source] = draft_wide[start : start + each, :].astype(bf16)
+
+            def send_partial(k, carry):
+                draft_push(q, lax.rem(me + k, n), me).start()
+                return carry
+
+            lax.fori_loop(1, n, send_partial, 0)
+            draft_returned[q, me] = draft_leaving[q, me]
+
+    for p in range(piece_count + 3):
         if p < piece_count:
             partial_step(p)
-        if 0 <= p - lag_plane < piece_count:
-            plane_step(p - lag_plane)
-        if 0 <= p - lag_home < piece_count:
-            home_step(p - lag_home)
-
-    def take(k, carry):
-        source = lax.rem(me + n - k, n)
-        push(
-            blocks.at[source], blocks.at[source], block_out_sem.at[source], block_in_sem.at[source], source
-        ).wait_recv()
-        block_rows[pl.ds(source, 1), :] = blocks[source]
-        return carry
-
-    block_rows[pl.ds(me, 1), :] = blocks[me]
-    lax.fori_loop(1, n, take, 0)
-    draft_rows = block_rows[...].astype(bf16)
-    for p in range(piece_count):
-        i = down_loads + p // stacked
-        fc_copy(p).wait()
-        first = p % stacked * depth
-        partial = jnp.dot(
-            draft_rows, weights[i % slots, first : first + depth, :], preferred_element_type=f32
-        )
-        for source in range(n):
-            line = partial[source : source + 1]
-            draft_leaving[source, p] = jnp.concatenate(
-                [line[:, :half], line[:, half:]], axis=0
-            ).astype(bf16)
-
-    def send_partial(k, carry):
-        peer = lax.rem(me + k, n)
-        push(
-            draft_leaving.at[peer],
-            draft_returned.at[me],
-            draft_out_sem.at[peer],
-            draft_in_sem.at[me],
-            peer,
-        ).start()
-        return carry
-
-    lax.fori_loop(1, n, send_partial, 0)
-    draft_returned[me] = draft_leaving[me]
+        if 0 <= p - 1 < piece_count:
+            core_step(p - 1)
+        if 0 <= p - 3 < piece_count:
+            chip_step(p - 3)
+        if 0 <= p - 5 < piece_count:
+            home_step(p - 5)
+    for p in range(max(0, piece_count - 2), piece_count - 1):
+        home_step(p)
+    ready = sent[0]
+    soon = (me < ready) | (me >= block_count)
+
+    @pl.when(soon)
+    def _():
+        draft_step()
+
+    home_step(piece_count - 1)
+
+    @pl.when(jnp.logical_not(soon))
+    def _():
+        draft_step()
 
     def drain(k, carry):
         peer = lax.rem(me + n - k, n)
-        push(
-            draft_leaving.at[peer],
-            draft_returned.at[peer],
-            draft_out_sem.at[peer],
-            draft_in_sem.at[peer],
-            peer,
-        ).wait()
+        for q in range(part_count):
+            draft_push(q, peer, peer).wait()
         return carry
 
     lax.fori_loop(1, n, drain, 0)
-    for p in range(piece_count):
-        total = draft_returned[0, p].astype(f32)
+    each = line_count // part_count
+    for q in range(part_count):
+        total = draft_returned[q, 0].astype(f32)
         for source in range(1, n):
-            total = total + draft_returned[source, p].astype(f32)
-        start = p * SLICE
-        draft_out[:, start : start + half] = total[0:1].astype(bf16)
-        draft_out[:, start + half : start + SLICE] = total[1:2].astype(bf16)
+            total = total + draft_returned[q, source].astype(f32)
+        draft_out[q * each : (q + 1) * each, :] = total
 
     for k in range(chunk_count):
         for step in range(1, EXPERTS):
             from_plane(k, step).wait_send()
-        for step in range(1, group):
-            in_plane(k, step).wait_send()
+        row_push(k, lane, 0, chip_peer).wait_send()
+        row_push(k, lane, 1, core_peer).wait_send()
+        row_push(k, chip_lane, 2, core_peer).wait_send()
     for p in range(piece_count):
-        for step in range(1, group):
-            from_member(p, step).wait_send()
+        core_push(p).wait_send()
+        chip_push(p).wait_send()
         for step in range(1, EXPERTS):
             from_expert(p, step).wait_send()
     for b in range(block_count):
         wait_block(picked, b, b)
         wait_block(embed_row, b, block_count + b)
+
+
+def finish_kernel(layer, draft_lines, layer_out, draft_out):
+    layer_out[...] = layer[...]
+    for t in range(draft_lines.shape[0]):
+        draft_out[:, t * LANES : (t + 1) * LANES] = draft_lines[t : t + 1, :].astype(jnp.bfloat16)
 
 
 def fused(
@@ -1055,69 +1091,77 @@
     depth = draft_fc.shape[0]
     group = n // EXPERTS
     share = EXPERTS * CAP
-    slots = 13
-    chunks = model_width // width
+    slots = 26
     pieces = model_width // SLICE
-    stacked = width // depth
-    loads = 2 * chunks * (width // SLICE) + pieces + -(-pieces // stacked)
+    halves = width // SLICE
+    parts = 3
+    loads = 2 * pieces * halves + pieces * halves + pieces
+    line_count = model_width // LANES
     kv_width = tree_key_value.shape[2]
-    key_rows = key_value_cache.shape[2] + 128
+    key_rows = key_value_cache.shape[2] + LANES
     anywhere = pl.BlockSpec(memory_space=pl.ANY)
     scalars = pl.BlockSpec(memory_space=pltpu.SMEM)
     whole = pl.BlockSpec(memory_space=pltpu.VMEM)
     bf16, f32 = jnp.bfloat16, jnp.float32
     dma = pltpu.SemaphoreType.DMA
-    return pl.pallas_call(
+    layer, draft_lines = pl.pallas_call(
         functools.partial(fused_kernel, n, slots),
         out_shape=(
             jax.ShapeDtypeStruct((TREE_NODES, model_width), bf16),
-            jax.ShapeDtypeStruct((1, model_width), bf16),
+            jax.ShapeDtypeStruct((line_count, LANES), f32),
         ),
         in_specs=[scalars] * 4 + [anywhere] * 11,
         out_specs=(whole, whole),
         scratch_shapes=[
-            pltpu.VMEM((slots, width, SLICE), bf16),
+            pltpu.VMEM((slots, SLICE, SLICE), bf16),
             pltpu.VMEM((TREE_NODES, model_width), bf16),
             pltpu.VMEM((TREE_NODES, 2, kv_width), bf16),
             pltpu.VMEM((key_rows, kv_width), bf16),
             pltpu.VMEM((key_rows, kv_width), bf16),
             pltpu.VMEM((TREE_NODES, model_width), bf16),
-            pltpu.VMEM((1, model_width), bf16),
+            pltpu.VMEM((line_count, LANES), bf16),
             pltpu.VMEM((EXPERTS, model_width), bf16),
             pltpu.VMEM((1, model_width), bf16),
             pltpu.VMEM((2, 16, kv_width), f32),
             pltpu.VMEM((8, model_width), f32),
             pltpu.VMEM((8, model_width), bf16),
-            pltpu.VMEM((chunks, EXPERTS, CAP, width), bf16),
-            pltpu.VMEM((chunks, EXPERTS, CAP, width), bf16),
-            pltpu.VMEM((chunks, group * share, width), bf16),
+            pltpu.VMEM((pieces, EXPERTS, CAP, SLICE), bf16),
+            pltpu.VMEM((pieces, EXPERTS, CAP, SLICE), bf16),
+            pltpu.VMEM((pieces, group * share, SLICE), bf16),
             pltpu.VMEM((group * share, width), f32),
             pltpu.VMEM((group * share, width), f32),
-            pltpu.VMEM((group * share, width), bf16),
-            pltpu.VMEM((pieces, group, share, SLICE), bf16),
-            pltpu.VMEM((pieces, group, share, SLICE), bf16),
+            pltpu.VMEM((halves, group * share, SLICE), bf16),
+            pltpu.VMEM((pieces, 2, share, SLICE), bf16),
+            pltpu.VMEM((pieces, 2, share, SLICE), bf16),
+            pltpu.VMEM((pieces, 2, share, SLICE), bf16),
+            pltpu.VMEM((pieces, share, SLICE), f32),
+            pltpu.VMEM((pieces, share, SLICE), bf16),
+            pltpu.VMEM((pieces, share, SLICE), bf16),
             pltpu.VMEM((pieces, EXPERTS, CAP, SLICE), bf16),
             pltpu.VMEM((pieces, EXPERTS, CAP, SLICE), bf16),
             pltpu.VMEM((1, model_width), f32),
             pltpu.VMEM((1, model_width), f32),
             pltpu.VMEM((n, 1, depth), f32),
             pltpu.VMEM((n, depth), f32),
-            pltpu.VMEM((n, pieces, 2, SLICE // 2), bf16),
-            pltpu.VMEM((n, pieces, 2, SLICE // 2), bf16),
-            dma((loads, stacked)),
+            pltpu.VMEM((n * line_count, LANES), f32),
+            pltpu.VMEM((parts, n, line_count // parts, LANES), bf16),
+            pltpu.VMEM((parts, n, line_count // parts, LANES), bf16),
+            dma((loads,)),
             dma((8,)),
-            dma((chunks, EXPERTS)),
-            dma((chunks, EXPERTS)),
-            dma((chunks, group)),
-            dma((chunks, group)),
-            dma((pieces, group)),
-            dma((pieces, group)),
+            dma((pieces, EXPERTS)),
+            dma((pieces, EXPERTS)),
+            dma((pieces, 3)),
+            dma((pieces, 3)),
+            dma((pieces,)),
+            dma((pieces,)),
+            dma((pieces,)),
+            dma((pieces,)),
             dma((pieces, EXPERTS)),
             dma((pieces, EXPERTS)),
             dma((n,)),
             dma((n,)),
-            dma((n,)),
-            dma((n,)),
+            dma((parts, n)),
+            dma((parts, n)),
         ],
         compiler_params=pltpu.CompilerParams(
             collective_id=0, has_side_effects=True, vmem_limit_bytes=67_000_000
@@ -1132,7 +1176,7 @@
         tree_key_value,
         key_value_cache,
         residual,
-        ffn_gain.reshape(1, model_width),
+        ffn_gain.reshape(line_count, LANES),
         router.T,
         next_embed,
         gate_weight,
@@ -1140,6 +1184,16 @@
         down_weight,
         draft_fc,
     )
+    return pl.pallas_call(
+        finish_kernel,
+        out_shape=(
+            jax.ShapeDtypeStruct((TREE_NODES, model_width), bf16),
+            jax.ShapeDtypeStruct((1, model_width), bf16),
+        ),
+        in_specs=[whole, whole],
+        out_specs=(whole, whole),
+        name="finish",
+    )(layer, draft_lines)
 
 
 def fits(lengths, gate_weight, draft_fc, n):
@@ -1147,15 +1201,12 @@
     depth = draft_fc.shape[0]
     return (
         lengths.shape[0] == 1
-        and n % EXPERTS == 0
-        and width % SLICE == 0
-        and model_width % width == 0
-        and model_width % SLICE == 0
-        and depth % 128 == 0
-        and width % depth <= width // 2
-        and depth <= width
+        and n == 4 * EXPERTS
+        and width == 2 * SLICE
+        and model_width == 6 * SLICE
+        and depth % LANES == 0
+        and depth <= SLICE
         and n * depth == 2 * model_width
-        and n * CAP <= 128
     )
 
 

time: 75.1 us -> 60.1 us (0.80)
  Pallas kernels: 68.7 us -> 58 us
  local copies, waits for them, and re-layouts: 4.24 us -> 0 us
    pallas_call x1, Pallas kernels: 68.7 us -> 56.4 us  [fused(): pl.pallas_call(functools.partial(fused_kernel, n, slots), out_shape=(jax....]
    unnamed x2 -> x0, local copies, waits for them, and re-layouts: 2.91 us -> none
    pallas_call x0 -> x1, Pallas kernels: none -> 1.57 us  [fused(): pl.pallas_call(finish_kernel, out_shape=(jax.ShapeDtypeStruct((TREE_NODES...]
    reshape x1 -> x0, local copies, waits for them, and re-layouts: 1.33 us -> none  [fused(): ffn_gain.reshape(1, model_width)]
where the time goes in v2:
time: 60.1 us; the launch traced here: 59.9 us
  Pallas kernels  58 us (97%)
  between operations  1.93 us (3%)
    pallas_call x1, Pallas kernels, fused(): pl.pallas_call(functools.partial(fused_kernel, n, slots), out_shape=(jax....  56.4 us
    pallas_call x1, Pallas kernels, fused(): pl.pallas_call(finish_kernel, out_shape=(jax.ShapeDtypeStruct((TREE_NODES...  1.57 us

profile of v2, /device:TPU:0, one launch (start us, length us, event | category | flops | bytes accessed | tf_op | source)
XLA Modules:
  0.0 59.9 jit_solution(8140486107090653711)
XLA Ops:
  1.9 56.4 %fused.1 = (bf16[6,6144]{1,0:T(8,128)(2,1)}, f32[48,128]{1,0:T(8,128)}) custom-call(s32[1]{0:T(128)S(6)} %copy.17.lengths, s32[6]{0:T(128)} %parents.1, s32[2,6]{1,0:T(2,128)} %bitcast.5, s32[1]{0:T(128)S(6)} %copy.18.accepted, bf16[6,6144]{1,0:T(8,128)(2,1)} %queries_hbm.1, bf16[6,2,1024]{2,1,0:T(2,128)(2,1)} %tree_hbm.1, ...), custom_call_target="tpu_custom_call" | custom-call | tf_op jit(solution)/shard_map/fused/pallas_call | solution.py:1107
  58.4 1.6 %finish.1 = (bf16[6,6144]{1,0:T(8,128)(2,1)}, bf16[1,6144]{1,0:T(2,128)(2,1)}) custom-call(bf16[6,6144]{1,0:T(8,128)(2,1)} %get-tuple-element.4.layer, f32[48,128]{1,0:T(8,128)} %get-tuple-element.5.draft_lines), custom_call_target="tpu_custom_call" | custom-call | tf_op jit(solution)/shard_map/finish/pallas_call | solution.py:1187

commit v3 on v2

--- a/solution.py
+++ b/solution.py
@@ -470,6 +470,7 @@
 
 SLICE = 1024
 LANES = 128
+UNIT = 256
 
 
 def greet_all(n, me):
@@ -529,10 +530,16 @@
     chip_returned,
     home_leaving,
     home_returned,
-    picked,
+    pick_rows,
+    pick_arrived,
+    shares,
+    share_leaving,
+    share_rows,
+    hidden_row,
     embed_row,
     blocks,
     block_rows,
+    draft_sum,
     draft_wide,
     draft_leaving,
     draft_returned,
@@ -548,6 +555,10 @@
     chip_in_sem,
     home_out_sem,
     home_in_sem,
+    pick_out_sem,
+    pick_in_sem,
+    share_out_sem,
+    share_in_sem,
     block_out_sem,
     block_in_sem,
     draft_out_sem,
@@ -565,9 +576,15 @@
     model_width = down_hbm.shape[1]
     width = down_hbm.shape[0]
     depth = fc_hbm.shape[0]
-    chunk_count = model_width // SLICE
+    slice_count = model_width // SLICE
     half_count = width // SLICE
-    piece_count = model_width // SLICE
+    half = SLICE // 2
+    chunks = [(0, half), (half, half)] + [(k * SLICE, SLICE) for k in range(1, slice_count)]
+    last = model_width - SLICE
+    pieces = [(k * SLICE, SLICE) for k in range(slice_count - 1)]
+    pieces += [(last, SLICE - UNIT), (model_width - UNIT, UNIT)]
+    piece_count = len(pieces)
+    unit_count = depth // UNIT
     block_count = model_width // depth
     padded = 8
     share = EXPERTS * CAP
@@ -578,12 +595,10 @@
     part_count = draft_leaving.shape[0]
 
     pairs = [
-        ("pair", k, h, i) for k in range(chunk_count) for h in range(half_count) for i in range(2)
+        ("pair", k, h, i) for k in range(slice_count) for h in range(half_count) for i in range(2)
     ]
     downs = [("down", p, a) for p in range(piece_count) for a in range(half_count)]
-    fcs = [("fc", p) for p in range(piece_count)]
-    early = len(downs) // 2
-    order = pairs + downs[:early] + fcs + downs[early:]
+    order = pairs + downs + [("fc", p) for p in range(slice_count)]
     place = {item: i for i, item in enumerate(order)}
 
     def load_copy(item):
@@ -594,8 +609,10 @@
             source = (gate_hbm, up_hbm)[item[3]]
             view = source.at[k * SLICE : (k + 1) * SLICE, h * SLICE : (h + 1) * SLICE]
         elif item[0] == "down":
-            p, a = item[1], item[2]
-            view = down_hbm.at[a * SLICE : (a + 1) * SLICE, p * SLICE : (p + 1) * SLICE]
+            a = item[2]
+            start, size = pieces[item[1]]
+            view = down_hbm.at[a * SLICE : (a + 1) * SLICE, start : start + size]
+            slot = weights.at[i % slots, :, 0:size]
         else:
             p = item[1]
             view = fc_hbm.at[:, p * SLICE : (p + 1) * SLICE]
@@ -728,41 +745,57 @@
             )
     placing = placing.astype(bf16)
 
-    pl.semaphore_wait(barrier, n - 1)
-
-    def to_plane(k, step):
+    def to_plane(c, step):
         plane = lax.rem(mine + step, EXPERTS)
+        cols = pl.ds(chunks[c][0], chunks[c][1])
         return push(
-            packed.at[k, plane],
-            arrived.at[k, mine],
-            out_sem.at[k, plane],
-            in_sem.at[k, mine],
+            packed.at[plane, :, cols],
+            arrived.at[mine, :, cols],
+            out_sem.at[c, plane],
+            in_sem.at[c, mine],
             plane * group + lane,
         )
 
-    def from_plane(k, step):
+    def from_plane(c, step):
         plane = lax.rem(mine + EXPERTS - step, EXPERTS)
+        cols = pl.ds(chunks[c][0], chunks[c][1])
         return push(
-            packed.at[k, plane],
-            arrived.at[k, plane],
-            out_sem.at[k, plane],
-            in_sem.at[k, plane],
+            packed.at[plane, :, cols],
+            arrived.at[plane, :, cols],
+            out_sem.at[c, plane],
+            in_sem.at[c, plane],
             plane * group + lane,
         )
 
-    for k in range(chunk_count):
-        cols = slice(k * SLICE, (k + 1) * SLICE)
-        gains = [gain[k * lines + t : k * lines + t + 1, :].astype(f32) for t in range(lines)]
+    def pack_step(c):
+        start, size = chunks[c]
+        cols = slice(start, start + size)
+        gains = [
+            gain[t : t + 1, :].astype(f32)
+            for t in range(start // LANES, (start + size) // LANES)
+        ]
         normal = (hidden[:, cols] * level * jnp.concatenate(gains, axis=1)).astype(bf16)
         normed[:, cols] = normal
         spread = jnp.dot(placing, normal, preferred_element_type=f32)
         for e in range(EXPERTS):
-            packed[k, e] = spread[e * padded : e * padded + CAP].astype(bf16)
+            packed[e, :, cols] = spread[e * padded : e * padded + CAP].astype(bf16)
+        arrived[mine, :, cols] = packed[mine, :, cols]
+
+    pack_step(0)
+    pl.semaphore_wait(barrier, n - 1)
+    for c in range(len(chunks)):
+        if c > 0:
+            pack_step(c)
         for step in range(1, EXPERTS):
-            to_plane(k, step).start()
-        arrived[k, mine] = packed[k, mine]
-
+            to_plane(c, step).start()
+
+    token_row = row8[:, 0:1]
     embed_row[...] = embed[...].astype(f32)
+    for k in range(slice_count):
+        cols = slice(k * SLICE, (k + 1) * SLICE)
+        hidden_row[:, cols] = jnp.sum(
+            jnp.where(token_row == accepted[0], hidden[:, cols], 0.0), axis=0, keepdims=True
+        )
 
     def block_push(row, b, j):
         source = row.at[:, b * depth : (b + 1) * depth]
@@ -784,9 +817,10 @@
 
     for b in range(block_count):
         send_block(embed_row, b, block_count + b)
+        send_block(hidden_row, b, b)
 
     logits = [jnp.zeros((padded, 1), f32) for _ in range(EXPERTS)]
-    for k in range(chunk_count):
+    for k in range(slice_count):
         cols = slice(k * SLICE, (k + 1) * SLICE)
         normal = normed[:, cols].astype(f32)
         for e in range(EXPERTS):
@@ -794,7 +828,6 @@
                 normal * router[e : e + 1, cols].astype(f32), axis=-1, keepdims=True
             )
     ids = [jnp.full((padded, 1), -1, jnp.int32) for _ in range(4)]
-    token_row = row8[:, 0:1]
     for token, choices in enumerate(places):
         for choice, (expert, rank) in enumerate(choices):
             ids[choice] = jnp.where(token_row == token, expert, ids[choice])
@@ -809,17 +842,44 @@
     weighted = jnp.where(share_col == ids[2], first_share, 0.0) + jnp.where(
         share_col == ids[3], 1.0 - first_share, 0.0
     )
-    high = weighted.astype(bf16).astype(f32)
-    middle = (weighted - high).astype(bf16).astype(f32)
-    low = weighted - high - middle
-    mixers = jnp.concatenate([high, middle, low], axis=0).astype(bf16)
-
-    def lane_rows(k, which):
-        return rows.at[k, pl.ds(pl.multiple_of(which * share, share), share), :]
-
-    def row_push(k, which, sem, peer):
-        block = lane_rows(k, which)
-        return push(block, block, plane_out_sem.at[k, sem], plane_in_sem.at[k, sem], peer)
+
+    def split(exact):
+        high = exact.astype(bf16).astype(f32)
+        middle = (exact - high).astype(bf16).astype(f32)
+        low = exact - high - middle
+        return jnp.concatenate([high, middle, low], axis=0).astype(bf16)
+
+    mixers = split(weighted)
+
+    def pick_push(step, back):
+        plane = lax.rem(mine + (EXPERTS - step if back else step), EXPERTS)
+        return push(
+            pick_rows.at[plane],
+            pick_arrived.at[plane if back else mine],
+            pick_out_sem.at[plane],
+            pick_in_sem.at[plane if back else mine],
+            plane * group + lane,
+        )
+
+    for e in range(EXPERTS):
+        chosen = jnp.zeros((padded, LANES), f32)
+        for expert, position, portion in (
+            (ids[0], ids[2], first_share),
+            (ids[1], ids[3], 1.0 - first_share),
+        ):
+            here = (col8 == mine * CAP + position - expert * CAP) & (expert == e)
+            chosen = chosen + jnp.where(here, portion, 0.0)
+        pick_rows[e] = jnp.sum(
+            jnp.where(token_row == accepted[0], chosen, 0.0), axis=0, keepdims=True
+        )
+    for step in range(1, EXPERTS):
+        pick_push(step, False).start()
+    pick_arrived[mine] = pick_rows[mine]
+
+    def row_push(c, which, sem, peer):
+        start, size = chunks[c]
+        block = rows.at[pl.ds(pl.multiple_of(which * share, share), share), pl.ds(start, size)]
+        return push(block, block, plane_out_sem.at[c, sem], plane_in_sem.at[c, sem], peer)
 
     chip_lane = (1 - across) * 2 + core
     core_lane = across * 2 + (1 - core)
@@ -828,8 +888,10 @@
     def gather_step(k):
         for step in range(1, EXPERTS):
             from_plane(k, step).wait_recv()
-        rows[k, pl.ds(pl.multiple_of(lane * share, share), share), :] = jnp.concatenate(
-            [arrived[k, s].astype(f32) for s in range(EXPERTS)], axis=0
+        start, size = chunks[k]
+        cols = slice(start, start + size)
+        rows[pl.ds(pl.multiple_of(lane * share, share), share), cols] = jnp.concatenate(
+            [arrived[s, :, cols].astype(f32) for s in range(EXPERTS)], axis=0
         ).astype(bf16)
         row_push(k, lane, 0, chip_peer).start()
         row_push(k, lane, 1, core_peer).start()
@@ -838,44 +900,60 @@
         row_push(k, chip_lane, 0, chip_peer).wait_recv()
         row_push(k, chip_lane, 2, core_peer).start()
 
-    def expert_step(k):
-        row_push(k, core_lane, 1, core_peer).wait_recv()
-        row_push(k, far_lane, 2, core_peer).wait_recv()
+    def expert_step(c):
+        row_push(c, core_lane, 1, core_peer).wait_recv()
+        row_push(c, far_lane, 2, core_peer).wait_recv()
+        start, size = chunks[c]
+        k, first = start // SLICE, start % SLICE
+        final = start + size == model_width
         for h in range(half_count):
             cols = slice(h * SLICE, (h + 1) * SLICE)
             sums = []
             for i, total in ((0, gate_sum), (1, up_sum)):
                 item = ("pair", k, h, i)
-                load_copy(item).wait()
+                if first == 0:
+                    load_copy(item).wait()
                 value = jnp.dot(
-                    rows[k], weights[place[item] % slots], preferred_element_type=f32
+                    rows[:, start : start + size],
+                    weights[place[item] % slots, first : first + size, :],
+                    preferred_element_type=f32,
                 )
-                if k > 0:
+                if start > 0:
                     value = value + total[:, cols]
-                if k < chunk_count - 1:
+                if not final:
                     total[:, cols] = value
                 sums.append(value)
-                start_load(place[item] + slots)
-            if k == chunk_count - 1:
+                if first + size == SLICE:
+                    start_load(place[item] + slots)
+            if final:
                 activation[h] = (jax.nn.silu(sums[0]) * sums[1]).astype(bf16)
 
-    for t in range(chunk_count + 6):
-        if t < chunk_count:
+    for t in range(len(chunks) + 3):
+        if t < len(chunks):
             gather_step(t)
-        if 0 <= t - 2 < chunk_count:
+        if 0 <= t - 2 < len(chunks):
             forward_step(t - 2)
-        if 0 <= t - 3 < chunk_count:
+        if 0 <= t - 3 < len(chunks):
             expert_step(t - 3)
 
+    def piece_cols(p):
+        return pl.ds(pieces[p][0], pieces[p][1])
+
     def core_push(p):
+        cols = piece_cols(p)
         return push(
-            leaving.at[p], returned.at[p], core_out_sem.at[p], core_in_sem.at[p], core_peer
+            leaving.at[:, :, cols],
+            returned.at[:, :, cols],
+            core_out_sem.at[p],
+            core_in_sem.at[p],
+            core_peer,
         )
 
     def chip_push(p):
+        cols = piece_cols(p)
         return push(
-            chip_leaving.at[p],
-            chip_returned.at[p],
+            chip_leaving.at[:, cols],
+            chip_returned.at[:, cols],
             chip_out_sem.at[p],
             chip_in_sem.at[p],
             chip_peer,
@@ -884,8 +962,8 @@
     def to_home(p, step):
         plane = lax.rem(mine + step, EXPERTS)
         return push(
-            home_leaving.at[p, plane],
-            home_returned.at[p, mine],
+            home_leaving.at[plane, :, piece_cols(p)],
+            home_returned.at[mine, :, piece_cols(p)],
             home_out_sem.at[p, plane],
             home_in_sem.at[p, mine],
             plane * group + lane,
@@ -894,20 +972,22 @@
     def from_expert(p, step):
         plane = lax.rem(mine + EXPERTS - step, EXPERTS)
         return push(
-            home_leaving.at[p, plane],
-            home_returned.at[p, plane],
+            home_leaving.at[plane, :, piece_cols(p)],
+            home_returned.at[plane, :, piece_cols(p)],
             home_out_sem.at[p, plane],
             home_in_sem.at[p, plane],
             plane * group + lane,
         )
 
     def partial_step(p):
+        start, size = pieces[p]
+        cols = slice(start, start + size)
         partial = None
         for a in range(half_count):
             item = ("down", p, a)
             load_copy(item).wait()
             value = jnp.dot(
-                activation[a], weights[place[item] % slots], preferred_element_type=f32
+                activation[a], weights[place[item] % slots, :, 0:size], preferred_element_type=f32
             )
             partial = value if partial is None else partial + value
             start_load(place[item] + slots)
@@ -917,49 +997,76 @@
 
             @pl.when(core == c)
             def _():
-                kept[p, a] = block
+                kept[a, :, cols] = block
 
             @pl.when(core != c)
             def _():
-                leaving[p, a] = block
+                leaving[a, :, cols] = block
 
         core_push(p).start()
 
     def core_step(p):
         core_push(p).wait_recv()
+        start, size = pieces[p]
+        cols = slice(start, start + size)
         far = 1 - across
-        chip_leaving[p] = (kept[p, far].astype(f32) + returned[p, far].astype(f32)).astype(bf16)
+        chip_leaving[:, cols] = (
+            kept[far, :, cols].astype(f32) + returned[far, :, cols].astype(f32)
+        ).astype(bf16)
         chip_push(p).start()
-        chip_sum[p] = kept[p, across].astype(f32) + returned[p, across].astype(f32)
-
-    def chip_step(p):
+        chip_sum[:, cols] = kept[across, :, cols].astype(f32) + returned[across, :, cols].astype(
+            f32
+        )
+
+    def share_push(unit, b):
+        part = unit % unit_count
+        return push(
+            share_leaving.at[unit],
+            shares.at[me, part],
+            share_out_sem.at[unit],
+            share_in_sem.at[me, part],
+            b,
+        )
+
+    def chip_step(p, pick_mixers):
         chip_push(p).wait_recv()
-        total = chip_sum[p] + chip_returned[p].astype(f32)
+        start, size = pieces[p]
+        cols = slice(start, start + size)
+        total = chip_sum[:, cols] + chip_returned[:, cols].astype(f32)
+        mixed = jnp.dot(pick_mixers, total.astype(bf16), preferred_element_type=f32)
+        portion = mixed[:padded] + mixed[padded : 2 * padded] + mixed[2 * padded :]
+        for unit in range(start // UNIT, (start + size) // UNIT):
+            b = unit // unit_count
+            first = unit * UNIT - start
+            value = portion[:EXPERTS, first : first + UNIT].astype(bf16)
+
+            @pl.when(me != b)
+            def _():
+                share_leaving[unit] = value
+                share_push(unit, b).start()
+
+            @pl.when(me == b)
+            def _():
+                shares[b, unit % unit_count] = value
+
         for s in range(EXPERTS):
-            home_leaving[p, s] = total[s * CAP : (s + 1) * CAP].astype(bf16)
+            home_leaving[s, :, cols] = total[s * CAP : (s + 1) * CAP].astype(bf16)
         for step in range(1, EXPERTS):
             to_home(p, step).start()
-        home_returned[p, mine] = home_leaving[p, mine]
-
-    sent = [0]
+        home_returned[mine, :, cols] = home_leaving[mine, :, cols]
 
     def home_step(p):
         for step in range(1, EXPERTS):
             from_expert(p, step).wait_recv()
-        cols = slice(p * SLICE, (p + 1) * SLICE)
+        start, size = pieces[p]
+        cols = slice(start, start + size)
         block = jnp.concatenate(
-            [home_returned[p, e].astype(f32) for e in range(EXPERTS)], axis=0
+            [home_returned[e, :, cols].astype(f32) for e in range(EXPERTS)], axis=0
         ).astype(bf16)
         mixed = jnp.dot(mixers, block, preferred_element_type=f32)
         expert_sum = mixed[:padded] + mixed[padded : 2 * padded] + mixed[2 * padded :]
         result = (hidden[:, cols] + expert_sum).astype(bf16)
         layer_out[:, cols] = result[:TREE_NODES]
-        picked[:, cols] = jnp.sum(
-            jnp.where(token_row == accepted[0], result.astype(f32), 0.0), axis=0, keepdims=True
-        )
-        while sent[0] < block_count and (sent[0] + 1) * depth <= (p + 1) * SLICE:
-            send_block(picked, sent[0], sent[0])
-            sent[0] += 1
 
     def draft_push(q, peer, at):
         return push(
@@ -970,7 +1077,10 @@
             peer,
         )
 
-    def draft_step():
+    def row_of(device):
+        return lax.rem(device, group) * EXPERTS + device // group
+
+    def block_step():
         def take(k, carry):
             source = lax.rem(me + n - k, n)
             push(
@@ -980,27 +1090,68 @@
                 block_in_sem.at[source],
                 source,
             ).wait_recv()
-            block_rows[pl.ds(source, 1), :] = blocks[source]
+            block_rows[pl.ds(row_of(source), 1), :] = blocks[source]
             return carry
 
-        block_rows[pl.ds(me, 1), :] = blocks[me]
+        block_rows[pl.ds(row_of(me), 1), :] = blocks[me]
         lax.fori_loop(1, n, take, 0)
-        draft_rows = block_rows[...].astype(bf16)
+        share_rows[...] = jnp.zeros_like(share_rows)
+
+    def share_step(first, past):
+        @pl.when(me < block_count)
+        def _():
+            for part in range(first, past):
+
+                def take(k, carry):
+                    source = lax.rem(me + n - k, n)
+                    push(
+                        shares.at[source, part],
+                        shares.at[source, part],
+                        share_out_sem.at[part],
+                        share_in_sem.at[source, part],
+                        source,
+                    ).wait_recv()
+                    return carry
+
+                lax.fori_loop(1, n, take, 0)
+                sums = []
+                for member in range(group):
+                    total = shares[member, part].astype(f32)
+                    for e in range(1, EXPERTS):
+                        total = total + shares[e * group + member, part].astype(f32)
+                    sums.append(total)
+                share_rows[:, part * UNIT : (part + 1) * UNIT] = jnp.concatenate(sums, axis=0)
+
+    def draft_step(first, past, final):
+        share_step(first, past)
+        deep = slice(first * UNIT, past * UNIT)
+        draft_rows = (block_rows[:, deep] + share_rows[:, deep]).astype(bf16)
+        per_part = slice_count // part_count
         for q in range(part_count):
-            for p in range(q * piece_count // part_count, (q + 1) * piece_count // part_count):
+            for p in range(q * per_part, (q + 1) * per_part):
                 item = ("fc", p)
-                load_copy(item).wait()
+                if first == 0:
+                    load_copy(item).wait()
                 partial = jnp.dot(
-                    draft_rows, weights[place[item] % slots, 0:depth, :], preferred_element_type=f32
+                    draft_rows, weights[place[item] % slots, deep, :], preferred_element_type=f32
                 )
+                cols = slice(p * SLICE, (p + 1) * SLICE)
+                if first > 0:
+                    partial = partial + draft_sum[:, cols]
+                if not final:
+                    draft_sum[:, cols] = partial
+                    continue
                 for t in range(lines):
                     draft_wide[pl.ds(p * lines + t, n, stride=line_count), :] = partial[
                         :, t * LANES : (t + 1) * LANES
                     ]
+            if not final:
+                continue
             each = line_count // part_count
-            for source in range(n):
-                start = source * line_count + q * each
-                draft_leaving[q, source] = draft_wide[start : start + each, :].astype(bf16)
+            for row in range(n):
+                device = row % EXPERTS * group + row // EXPERTS
+                start = row * line_count + q * each
+                draft_leaving[q, device] = draft_wide[start : start + each, :].astype(bf16)
 
             def send_partial(k, carry):
                 draft_push(q, lax.rem(me + k, n), me).start()
@@ -1008,30 +1159,51 @@
 
             lax.fori_loop(1, n, send_partial, 0)
             draft_returned[q, me] = draft_leaving[q, me]
+
+    for step in range(1, EXPERTS):
+        pick_push(step, True).wait_recv()
+    picks = jnp.concatenate(
+        [pick_arrived[s][:, :share] for s in range(EXPERTS)]
+        + [jnp.zeros((padded - EXPERTS, share), f32)],
+        axis=0,
+    )
+    pick_mixers = split(picks)
 
     for p in range(piece_count + 3):
         if p < piece_count:
             partial_step(p)
         if 0 <= p - 1 < piece_count:
             core_step(p - 1)
+        if p == piece_count:
+            block_step()
         if 0 <= p - 3 < piece_count:
-            chip_step(p - 3)
-        if 0 <= p - 5 < piece_count:
-            home_step(p - 5)
-    for p in range(max(0, piece_count - 2), piece_count - 1):
+            chip_step(p - 3, pick_mixers)
+    draft_step(0, unit_count - 1, False)
+    draft_step(unit_count - 1, unit_count, True)
+    for p in range(piece_count):
         home_step(p)
-    ready = sent[0]
-    soon = (me < ready) | (me >= block_count)
-
-    @pl.when(soon)
-    def _():
-        draft_step()
-
-    home_step(piece_count - 1)
-
-    @pl.when(jnp.logical_not(soon))
-    def _():
-        draft_step()
+
+    for c in range(len(chunks)):
+        for step in range(1, EXPERTS):
+            from_plane(c, step).wait_send()
+        row_push(c, lane, 0, chip_peer).wait_send()
+        row_push(c, lane, 1, core_peer).wait_send()
+        row_push(c, chip_lane, 2, core_peer).wait_send()
+    for step in range(1, EXPERTS):
+        pick_push(step, False).wait_send()
+    for p in range(piece_count):
+        core_push(p).wait_send()
+        chip_push(p).wait_send()
+        for step in range(1, EXPERTS):
+            from_expert(p, step).wait_send()
+    for b in range(block_count):
+        wait_block(hidden_row, b, b)
+        wait_block(embed_row, b, block_count + b)
+
+        @pl.when(me != b)
+        def _():
+            for part in range(unit_count):
+                share_push(b * unit_count + part, b).wait_send()
 
     def drain(k, carry):
         peer = lax.rem(me + n - k, n)
@@ -1046,21 +1218,6 @@
         for source in range(1, n):
             total = total + draft_returned[q, source].astype(f32)
         draft_out[q * each : (q + 1) * each, :] = total
-
-    for k in range(chunk_count):
-        for step in range(1, EXPERTS):
-            from_plane(k, step).wait_send()
-        row_push(k, lane, 0, chip_peer).wait_send()
-        row_push(k, lane, 1, core_peer).wait_send()
-        row_push(k, chip_lane, 2, core_peer).wait_send()
-    for p in range(piece_count):
-        core_push(p).wait_send()
-        chip_push(p).wait_send()
-        for step in range(1, EXPERTS):
-            from_expert(p, step).wait_send()
-    for b in range(block_count):
-        wait_block(picked, b, b)
-        wait_block(embed_row, b, block_count + b)
 
 
 def finish_kernel(layer, draft_lines, layer_out, draft_out):
@@ -1092,10 +1249,13 @@
     group = n // EXPERTS
     share = EXPERTS * CAP
     slots = 26
-    pieces = model_width // SLICE
+    slices = model_width // SLICE
     halves = width // SLICE
     parts = 3
-    loads = 2 * pieces * halves + pieces * halves + pieces
+    pieces = slices + 1
+    chunks = slices + 1
+    units = depth // UNIT
+    loads = 2 * slices * halves + pieces * halves + slices
     line_count = model_width // LANES
     kv_width = tree_key_value.shape[2]
     key_rows = key_value_cache.shape[2] + LANES
@@ -1125,46 +1285,56 @@
             pltpu.VMEM((2, 16, kv_width), f32),
             pltpu.VMEM((8, model_width), f32),
             pltpu.VMEM((8, model_width), bf16),
-            pltpu.VMEM((pieces, EXPERTS, CAP, SLICE), bf16),
-            pltpu.VMEM((pieces, EXPERTS, CAP, SLICE), bf16),
-            pltpu.VMEM((pieces, group * share, SLICE), bf16),
+            pltpu.VMEM((EXPERTS, CAP, model_width), bf16),
+            pltpu.VMEM((EXPERTS, CAP, model_width), bf16),
+            pltpu.VMEM((group * share, model_width), bf16),
             pltpu.VMEM((group * share, width), f32),
             pltpu.VMEM((group * share, width), f32),
             pltpu.VMEM((halves, group * share, SLICE), bf16),
-            pltpu.VMEM((pieces, 2, share, SLICE), bf16),
-            pltpu.VMEM((pieces, 2, share, SLICE), bf16),
-            pltpu.VMEM((pieces, 2, share, SLICE), bf16),
-            pltpu.VMEM((pieces, share, SLICE), f32),
-            pltpu.VMEM((pieces, share, SLICE), bf16),
-            pltpu.VMEM((pieces, share, SLICE), bf16),
-            pltpu.VMEM((pieces, EXPERTS, CAP, SLICE), bf16),
-            pltpu.VMEM((pieces, EXPERTS, CAP, SLICE), bf16),
+            pltpu.VMEM((2, share, model_width), bf16),
+            pltpu.VMEM((2, share, model_width), bf16),
+            pltpu.VMEM((2, share, model_width), bf16),
+            pltpu.VMEM((share, model_width), f32),
+            pltpu.VMEM((share, model_width), bf16),
+            pltpu.VMEM((share, model_width), bf16),
+            pltpu.VMEM((EXPERTS, CAP, model_width), bf16),
+            pltpu.VMEM((EXPERTS, CAP, model_width), bf16),
+            pltpu.VMEM((EXPERTS, 1, LANES), f32),
+            pltpu.VMEM((EXPERTS, 1, LANES), f32),
+            pltpu.VMEM((n, units, EXPERTS, UNIT), bf16),
+            pltpu.VMEM((model_width // UNIT, EXPERTS, UNIT), bf16),
+            pltpu.VMEM((n, depth), f32),
             pltpu.VMEM((1, model_width), f32),
             pltpu.VMEM((1, model_width), f32),
             pltpu.VMEM((n, 1, depth), f32),
             pltpu.VMEM((n, depth), f32),
+            pltpu.VMEM((n, model_width), f32),
             pltpu.VMEM((n * line_count, LANES), f32),
             pltpu.VMEM((parts, n, line_count // parts, LANES), bf16),
             pltpu.VMEM((parts, n, line_count // parts, LANES), bf16),
             dma((loads,)),
             dma((8,)),
-            dma((pieces, EXPERTS)),
-            dma((pieces, EXPERTS)),
-            dma((pieces, 3)),
-            dma((pieces, 3)),
+            dma((chunks, EXPERTS)),
+            dma((chunks, EXPERTS)),
+            dma((chunks, 3)),
+            dma((chunks, 3)),
             dma((pieces,)),
             dma((pieces,)),
             dma((pieces,)),
             dma((pieces,)),
             dma((pieces, EXPERTS)),
             dma((pieces, EXPERTS)),
+            dma((EXPERTS,)),
+            dma((EXPERTS,)),
+            dma((model_width // UNIT,)),
+            dma((n, units)),
             dma((n,)),
             dma((n,)),
             dma((parts, n)),
             dma((parts, n)),
         ],
         compiler_params=pltpu.CompilerParams(
-            collective_id=0, has_side_effects=True, vmem_limit_bytes=67_000_000
+            collective_id=0, has_side_effects=True, vmem_limit_bytes=66_000_000
         ),
         name="fused",
     )(
@@ -1204,7 +1374,8 @@
         and n == 4 * EXPERTS
         and width == 2 * SLICE
         and model_width == 6 * SLICE
-        and depth % LANES == 0
+        and depth % UNIT == 0
+        and depth > UNIT
         and depth <= SLICE
         and n * depth == 2 * model_width
     )

time: 60.1 us -> 52.6 us (0.88)
  Pallas kernels: 58 us -> 50.4 us
    pallas_call x1, Pallas kernels: 56.4 us -> 48.8 us  [fused(): pl.pallas_call(functools.partial(fused_kernel, n, slots), out_shape=(jax....]
where the time goes in v3:
time: 52.6 us; the launch traced here: 52.4 us
  Pallas kernels  50.4 us (96%)
  between operations  1.93 us (4%)
    pallas_call x1, Pallas kernels, fused(): pl.pallas_call(functools.partial(fused_kernel, n, slots), out_shape=(jax....  48.8 us
    pallas_call x1, Pallas kernels, fused(): pl.pallas_call(finish_kernel, out_shape=(jax.ShapeDtypeStruct((TREE_NODES...  1.57 us

profile of v3, /device:TPU:0, one launch (start us, length us, event | category | flops | bytes accessed | tf_op | source)
XLA Modules:
  0.0 52.4 jit_solution(15471428212541316378)
XLA Ops:
  1.9 48.8 %fused.1 = (bf16[6,6144]{1,0:T(8,128)(2,1)}, f32[48,128]{1,0:T(8,128)}) custom-call(s32[1]{0:T(128)S(6)} %copy.17.lengths, s32[6]{0:T(128)} %parents.1, s32[2,6]{1,0:T(2,128)} %bitcast.5, s32[1]{0:T(128)S(6)} %copy.18.accepted, bf16[6,6144]{1,0:T(8,128)(2,1)} %queries_hbm.1, bf16[6,2,1024]{2,1,0:T(2,128)(2,1)} %tree_hbm.1, ...), custom_call_target="tpu_custom_call" | custom-call | tf_op jit(solution)/shard_map/fused/pallas_call | solution.py:1267
  50.8 1.6 %finish.1 = (bf16[6,6144]{1,0:T(8,128)(2,1)}, bf16[1,6144]{1,0:T(2,128)(2,1)}) custom-call(bf16[6,6144]{1,0:T(8,128)(2,1)} %get-tuple-element.4.layer, f32[48,128]{1,0:T(8,128)} %get-tuple-element.5.draft_lines), custom_call_target="tpu_custom_call" | custom-call | tf_op jit(solution)/shard_map/finish/pallas_call | solution.py:1357

commit v4 on v3

--- a/solution.py
+++ b/solution.py
@@ -487,10 +487,10 @@
 def fused_kernel(
     n,
     slots,
-    lengths,
-    parents,
-    routes,
-    accepted,
+    lengths_hbm,
+    parents_hbm,
+    routes_hbm,
+    accepted_hbm,
     queries_hbm,
     tree_hbm,
     cache_hbm,
@@ -504,6 +504,10 @@
     fc_hbm,
     layer_out,
     draft_out,
+    lengths,
+    parents,
+    routes,
+    accepted,
     weights,
     queries,
     tree,
@@ -600,6 +604,23 @@
     downs = [("down", p, a) for p in range(piece_count) for a in range(half_count)]
     order = pairs + downs + [("fc", p) for p in range(slice_count)]
     place = {item: i for i, item in enumerate(order)}
+    sem_count = load_sem.shape[0]
+
+    def load_group(item):
+        if item[0] == "pair":
+            return item[1]
+        if item[0] == "down":
+            return slice_count + item[1]
+        return slice_count + piece_count
+
+    def wait_loads(item):
+        if item[0] == "pair":
+            view = weights.at[0 : 2 * half_count]
+        elif item[0] == "down":
+            view = weights.at[0:half_count, :, 0 : pieces[item[1]][1]]
+        else:
+            view = weights.at[0:slice_count, 0:depth, :]
+        pltpu.make_async_copy(view, view, load_sem.at[load_group(item) % sem_count]).wait()
 
     def load_copy(item):
         i = place[item]
@@ -617,7 +638,7 @@
             p = item[1]
             view = fc_hbm.at[:, p * SLICE : (p + 1) * SLICE]
             slot = weights.at[i % slots, 0:depth, :]
-        return pltpu.make_async_copy(view, slot, load_sem.at[i])
+        return pltpu.make_async_copy(view, slot, load_sem.at[load_group(item) % sem_count])
 
     def start_load(i):
         if i < len(order):
@@ -635,12 +656,18 @@
                 (gain_hbm, gain),
                 (router_hbm, router),
                 (embed_hbm, embed),
+                (lengths_hbm, lengths),
+                (parents_hbm, parents),
+                (routes_hbm, routes),
+                (accepted_hbm, accepted),
             ]
         )
     ]
-    for copy in inputs:
+    for copy in inputs[8:] + inputs[:8]:
         copy.start()
     barrier = greet_all(n, me)
+    for copy in inputs[8:]:
+        copy.wait()
 
     row8 = lax.broadcasted_iota(jnp.int32, (padded, LANES), 0)
     col8 = lax.broadcasted_iota(jnp.int32, (padded, LANES), 1)
@@ -731,7 +758,7 @@
             )
             hidden[:, cols] = state
             square = square + state * state
-    for copy in inputs[5:]:
+    for copy in inputs[5:8]:
         copy.wait()
     level = lax.rsqrt(jnp.sum(square, axis=-1, keepdims=True) / model_width + EPSILON)
 
@@ -751,21 +778,13 @@
         return push(
             packed.at[plane, :, cols],
             arrived.at[mine, :, cols],
-            out_sem.at[c, plane],
-            in_sem.at[c, mine],
+            out_sem,
+            in_sem.at[c],
             plane * group + lane,
         )
 
-    def from_plane(c, step):
-        plane = lax.rem(mine + EXPERTS - step, EXPERTS)
-        cols = pl.ds(chunks[c][0], chunks[c][1])
-        return push(
-            packed.at[plane, :, cols],
-            arrived.at[plane, :, cols],
-            out_sem.at[c, plane],
-            in_sem.at[c, plane],
-            plane * group + lane,
-        )
+    def awaited(ref, sem):
+        return push(ref, ref, sem, sem, core_peer)
 
     def pack_step(c):
         start, size = chunks[c]
@@ -799,7 +818,7 @@
 
     def block_push(row, b, j):
         source = row.at[:, b * depth : (b + 1) * depth]
-        return push(source, blocks.at[me], block_out_sem.at[j], block_in_sem.at[me], j)
+        return push(source, blocks.at[me], block_out_sem, block_in_sem, j)
 
     def send_block(row, b, j):
         @pl.when(me != j)
@@ -809,11 +828,6 @@
         @pl.when(me == j)
         def _():
             blocks[j] = row[:, b * depth : (b + 1) * depth]
-
-    def wait_block(row, b, j):
-        @pl.when(me != j)
-        def _():
-            block_push(row, b, j).wait_send()
 
     for b in range(block_count):
         send_block(embed_row, b, block_count + b)
@@ -851,13 +865,13 @@
 
     mixers = split(weighted)
 
-    def pick_push(step, back):
-        plane = lax.rem(mine + (EXPERTS - step if back else step), EXPERTS)
+    def pick_push(step):
+        plane = lax.rem(mine + step, EXPERTS)
         return push(
             pick_rows.at[plane],
-            pick_arrived.at[plane if back else mine],
-            pick_out_sem.at[plane],
-            pick_in_sem.at[plane if back else mine],
+            pick_arrived.at[mine],
+            pick_out_sem,
+            pick_in_sem,
             plane * group + lane,
         )
 
@@ -873,23 +887,20 @@
             jnp.where(token_row == accepted[0], chosen, 0.0), axis=0, keepdims=True
         )
     for step in range(1, EXPERTS):
-        pick_push(step, False).start()
+        pick_push(step).start()
     pick_arrived[mine] = pick_rows[mine]
 
     def row_push(c, which, sem, peer):
         start, size = chunks[c]
         block = rows.at[pl.ds(pl.multiple_of(which * share, share), share), pl.ds(start, size)]
-        return push(block, block, plane_out_sem.at[c, sem], plane_in_sem.at[c, sem], peer)
+        return push(block, block, plane_out_sem, plane_in_sem.at[c, sem], peer)
 
     chip_lane = (1 - across) * 2 + core
-    core_lane = across * 2 + (1 - core)
-    far_lane = (1 - across) * 2 + (1 - core)
 
     def gather_step(k):
-        for step in range(1, EXPERTS):
-            from_plane(k, step).wait_recv()
         start, size = chunks[k]
         cols = slice(start, start + size)
+        awaited(arrived.at[0 : EXPERTS - 1, :, pl.ds(start, size)], in_sem.at[k]).wait_recv()
         rows[pl.ds(pl.multiple_of(lane * share, share), share), cols] = jnp.concatenate(
             [arrived[s, :, cols].astype(f32) for s in range(EXPERTS)], axis=0
         ).astype(bf16)
@@ -898,21 +909,21 @@
 
     def forward_step(k):
         row_push(k, chip_lane, 0, chip_peer).wait_recv()
-        row_push(k, chip_lane, 2, core_peer).start()
+        row_push(k, chip_lane, 1, core_peer).start()
 
     def expert_step(c):
-        row_push(c, core_lane, 1, core_peer).wait_recv()
-        row_push(c, far_lane, 2, core_peer).wait_recv()
         start, size = chunks[c]
+        pair_rows = rows.at[0 : 2 * share, pl.ds(start, size)]
+        awaited(pair_rows, plane_in_sem.at[c, 1]).wait_recv()
         k, first = start // SLICE, start % SLICE
         final = start + size == model_width
+        if first == 0:
+            wait_loads(("pair", k))
         for h in range(half_count):
             cols = slice(h * SLICE, (h + 1) * SLICE)
             sums = []
             for i, total in ((0, gate_sum), (1, up_sum)):
                 item = ("pair", k, h, i)
-                if first == 0:
-                    load_copy(item).wait()
                 value = jnp.dot(
                     rows[:, start : start + size],
                     weights[place[item] % slots, first : first + size, :],
@@ -944,7 +955,7 @@
         return push(
             leaving.at[:, :, cols],
             returned.at[:, :, cols],
-            core_out_sem.at[p],
+            core_out_sem,
             core_in_sem.at[p],
             core_peer,
         )
@@ -954,7 +965,7 @@
         return push(
             chip_leaving.at[:, cols],
             chip_returned.at[:, cols],
-            chip_out_sem.at[p],
+            chip_out_sem,
             chip_in_sem.at[p],
             chip_peer,
         )
@@ -964,18 +975,8 @@
         return push(
             home_leaving.at[plane, :, piece_cols(p)],
             home_returned.at[mine, :, piece_cols(p)],
-            home_out_sem.at[p, plane],
-            home_in_sem.at[p, mine],
-            plane * group + lane,
-        )
-
-    def from_expert(p, step):
-        plane = lax.rem(mine + EXPERTS - step, EXPERTS)
-        return push(
-            home_leaving.at[plane, :, piece_cols(p)],
-            home_returned.at[plane, :, piece_cols(p)],
-            home_out_sem.at[p, plane],
-            home_in_sem.at[p, plane],
+            home_out_sem,
+            home_in_sem,
             plane * group + lane,
         )
 
@@ -983,9 +984,9 @@
         start, size = pieces[p]
         cols = slice(start, start + size)
         partial = None
+        wait_loads(("down", p))
         for a in range(half_count):
             item = ("down", p, a)
-            load_copy(item).wait()
             value = jnp.dot(
                 activation[a], weights[place[item] % slots, :, 0:size], preferred_element_type=f32
             )
@@ -1022,9 +1023,9 @@
         part = unit % unit_count
         return push(
             share_leaving.at[unit],
-            shares.at[me, part],
-            share_out_sem.at[unit],
-            share_in_sem.at[me, part],
+            shares.at[part, me],
+            share_out_sem,
+            share_in_sem.at[part // (unit_count - 1)],
             b,
         )
 
@@ -1047,7 +1048,7 @@
 
             @pl.when(me == b)
             def _():
-                shares[b, unit % unit_count] = value
+                shares[unit % unit_count, b] = value
 
         for s in range(EXPERTS):
             home_leaving[s, :, cols] = total[s * CAP : (s + 1) * CAP].astype(bf16)
@@ -1056,8 +1057,6 @@
         home_returned[mine, :, cols] = home_leaving[mine, :, cols]
 
     def home_step(p):
-        for step in range(1, EXPERTS):
-            from_expert(p, step).wait_recv()
         start, size = pieces[p]
         cols = slice(start, start + size)
         block = jnp.concatenate(
@@ -1072,8 +1071,8 @@
         return push(
             draft_leaving.at[q, peer],
             draft_returned.at[q, at],
-            draft_out_sem.at[q, peer],
-            draft_in_sem.at[q, at],
+            draft_out_sem,
+            draft_in_sem,
             peer,
         )
 
@@ -1081,44 +1080,26 @@
         return lax.rem(device, group) * EXPERTS + device // group
 
     def block_step():
-        def take(k, carry):
-            source = lax.rem(me + n - k, n)
-            push(
-                blocks.at[source],
-                blocks.at[source],
-                block_out_sem.at[source],
-                block_in_sem.at[source],
-                source,
-            ).wait_recv()
+        awaited(blocks.at[0 : n - 1], block_in_sem).wait_recv()
+
+        def take(source, carry):
             block_rows[pl.ds(row_of(source), 1), :] = blocks[source]
             return carry
 
-        block_rows[pl.ds(row_of(me), 1), :] = blocks[me]
-        lax.fori_loop(1, n, take, 0)
+        lax.fori_loop(0, n, take, 0)
         share_rows[...] = jnp.zeros_like(share_rows)
 
     def share_step(first, past):
         @pl.when(me < block_count)
         def _():
+            sem = share_in_sem.at[first // (unit_count - 1)]
+            awaited(shares.at[first:past, 0 : n - 1], sem).wait_recv()
             for part in range(first, past):
-
-                def take(k, carry):
-                    source = lax.rem(me + n - k, n)
-                    push(
-                        shares.at[source, part],
-                        shares.at[source, part],
-                        share_out_sem.at[part],
-                        share_in_sem.at[source, part],
-                        source,
-                    ).wait_recv()
-                    return carry
-
-                lax.fori_loop(1, n, take, 0)
                 sums = []
                 for member in range(group):
-                    total = shares[member, part].astype(f32)
+                    total = shares[part, member].astype(f32)
                     for e in range(1, EXPERTS):
-                        total = total + shares[e * group + member, part].astype(f32)
+                        total = total + shares[part, e * group + member].astype(f32)
                     sums.append(total)
                 share_rows[:, part * UNIT : (part + 1) * UNIT] = jnp.concatenate(sums, axis=0)
 
@@ -1127,11 +1108,11 @@
         deep = slice(first * UNIT, past * UNIT)
         draft_rows = (block_rows[:, deep] + share_rows[:, deep]).astype(bf16)
         per_part = slice_count // part_count
+        if first == 0:
+            wait_loads(("fc",))
         for q in range(part_count):
             for p in range(q * per_part, (q + 1) * per_part):
                 item = ("fc", p)
-                if first == 0:
-                    load_copy(item).wait()
                 partial = jnp.dot(
                     draft_rows, weights[place[item] % slots, deep, :], preferred_element_type=f32
                 )
@@ -1160,8 +1141,7 @@
             lax.fori_loop(1, n, send_partial, 0)
             draft_returned[q, me] = draft_leaving[q, me]
 
-    for step in range(1, EXPERTS):
-        pick_push(step, True).wait_recv()
+    awaited(pick_arrived.at[0 : EXPERTS - 1], pick_in_sem).wait_recv()
     picks = jnp.concatenate(
         [pick_arrived[s][:, :share] for s in range(EXPERTS)]
         + [jnp.zeros((padded - EXPERTS, share), f32)],
@@ -1180,38 +1160,29 @@
             chip_step(p - 3, pick_mixers)
     draft_step(0, unit_count - 1, False)
     draft_step(unit_count - 1, unit_count, True)
+    awaited(home_returned.at[0 : EXPERTS - 1], home_in_sem).wait_recv()
     for p in range(piece_count):
         home_step(p)
 
-    for c in range(len(chunks)):
-        for step in range(1, EXPERTS):
-            from_plane(c, step).wait_send()
-        row_push(c, lane, 0, chip_peer).wait_send()
-        row_push(c, lane, 1, core_peer).wait_send()
-        row_push(c, chip_lane, 2, core_peer).wait_send()
-    for step in range(1, EXPERTS):
-        pick_push(step, False).wait_send()
-    for p in range(piece_count):
-        core_push(p).wait_send()
-        chip_push(p).wait_send()
-        for step in range(1, EXPERTS):
-            from_expert(p, step).wait_send()
-    for b in range(block_count):
-        wait_block(hidden_row, b, b)
-        wait_block(embed_row, b, block_count + b)
-
-        @pl.when(me != b)
-        def _():
-            for part in range(unit_count):
-                share_push(b * unit_count + part, b).wait_send()
-
-    def drain(k, carry):
-        peer = lax.rem(me + n - k, n)
-        for q in range(part_count):
-            draft_push(q, peer, peer).wait()
-        return carry
-
-    lax.fori_loop(1, n, drain, 0)
+    awaited(packed.at[0 : EXPERTS - 1], out_sem).wait_send()
+    awaited(rows.at[0 : 3 * share, :], plane_out_sem).wait_send()
+    awaited(pick_rows.at[0 : EXPERTS - 1], pick_out_sem).wait_send()
+    awaited(leaving, core_out_sem).wait_send()
+    awaited(chip_leaving, chip_out_sem).wait_send()
+    awaited(home_leaving.at[0 : EXPERTS - 1], home_out_sem).wait_send()
+    awaited(blocks.at[0 : n - 1], block_out_sem).wait_send()
+    unit_total = share_leaving.shape[0]
+
+    @pl.when(me < block_count)
+    def _():
+        awaited(share_leaving.at[0 : unit_total - unit_count], share_out_sem).wait_send()
+
+    @pl.when(me >= block_count)
+    def _():
+        awaited(share_leaving, share_out_sem).wait_send()
+
+    awaited(draft_leaving.at[:, 0 : n - 1], draft_out_sem).wait_send()
+    awaited(draft_returned.at[:, 0 : n - 1], draft_in_sem).wait_recv()
     each = line_count // part_count
     for q in range(part_count):
         total = draft_returned[q, 0].astype(f32)
@@ -1248,19 +1219,17 @@
     depth = draft_fc.shape[0]
     group = n // EXPERTS
     share = EXPERTS * CAP
-    slots = 26
+    slots = 24
     slices = model_width // SLICE
     halves = width // SLICE
     parts = 3
     pieces = slices + 1
     chunks = slices + 1
     units = depth // UNIT
-    loads = 2 * slices * halves + pieces * halves + slices
     line_count = model_width // LANES
     kv_width = tree_key_value.shape[2]
     key_rows = key_value_cache.shape[2] + LANES
     anywhere = pl.BlockSpec(memory_space=pl.ANY)
-    scalars = pl.BlockSpec(memory_space=pltpu.SMEM)
     whole = pl.BlockSpec(memory_space=pltpu.VMEM)
     bf16, f32 = jnp.bfloat16, jnp.float32
     dma = pltpu.SemaphoreType.DMA
@@ -1270,9 +1239,13 @@
             jax.ShapeDtypeStruct((TREE_NODES, model_width), bf16),
             jax.ShapeDtypeStruct((line_count, LANES), f32),
         ),
-        in_specs=[scalars] * 4 + [anywhere] * 11,
+        in_specs=[anywhere] * 15,
         out_specs=(whole, whole),
         scratch_shapes=[
+            pltpu.SMEM(lengths.shape, jnp.int32),
+            pltpu.SMEM(parents.shape, jnp.int32),
+            pltpu.SMEM(routes.T.shape, jnp.int32),
+            pltpu.SMEM(accepted.shape, jnp.int32),
             pltpu.VMEM((slots, SLICE, SLICE), bf16),
             pltpu.VMEM((TREE_NODES, model_width), bf16),
             pltpu.VMEM((TREE_NODES, 2, kv_width), bf16),
@@ -1301,7 +1274,7 @@
             pltpu.VMEM((EXPERTS, CAP, model_width), bf16),
             pltpu.VMEM((EXPERTS, 1, LANES), f32),
             pltpu.VMEM((EXPERTS, 1, LANES), f32),
-            pltpu.VMEM((n, units, EXPERTS, UNIT), bf16),
+            pltpu.VMEM((units, n, EXPERTS, UNIT), bf16),
             pltpu.VMEM((model_width // UNIT, EXPERTS, UNIT), bf16),
             pltpu.VMEM((n, depth), f32),
             pltpu.VMEM((1, model_width), f32),
@@ -1312,29 +1285,29 @@
             pltpu.VMEM((n * line_count, LANES), f32),
             pltpu.VMEM((parts, n, line_count // parts, LANES), bf16),
             pltpu.VMEM((parts, n, line_count // parts, LANES), bf16),
-            dma((loads,)),
-            dma((8,)),
-            dma((chunks, EXPERTS)),
-            dma((chunks, EXPERTS)),
-            dma((chunks, 3)),
-            dma((chunks, 3)),
+            dma((10,)),
+            dma((12,)),
+            dma,
+            dma((chunks,)),
+            dma,
+            dma((chunks, 2)),
+            dma,
             dma((pieces,)),
+            dma,
             dma((pieces,)),
-            dma((pieces,)),
-            dma((pieces,)),
-            dma((pieces, EXPERTS)),
-            dma((pieces, EXPERTS)),
-            dma((EXPERTS,)),
-            dma((EXPERTS,)),
-            dma((model_width // UNIT,)),
-            dma((n, units)),
-            dma((n,)),
-            dma((n,)),
-            dma((parts, n)),
-            dma((parts, n)),
+            dma,
+            dma,
+            dma,
+            dma,
+            dma,
+            dma((2,)),
+            dma,
+            dma,
+            dma,
+            dma,
         ],
         compiler_params=pltpu.CompilerParams(
-            collective_id=0, has_side_effects=True, vmem_limit_bytes=66_000_000
+            collective_id=0, has_side_effects=True, vmem_limit_bytes=62_000_000
         ),
         name="fused",
     )(

time: 52.6 us -> 47.2 us (0.90)
  Pallas kernels: 50.4 us -> 45.1 us
    pallas_call x1, Pallas kernels: 48.8 us -> 43.5 us  [fused(): pl.pallas_call(functools.partial(fused_kernel, n, slots), out_shape=(jax....]
where the time goes in v4:
time: 47.2 us; the launch traced here: 47.1 us
  Pallas kernels  45.1 us (96%)
  between operations  1.93 us (4%)
    pallas_call x1, Pallas kernels, fused(): pl.pallas_call(functools.partial(fused_kernel, n, slots), out_shape=(jax....  43.5 us
    pallas_call x1, Pallas kernels, fused(): pl.pallas_call(finish_kernel, out_shape=(jax.ShapeDtypeStruct((TREE_NODES...  1.57 us

profile of v4, /device:TPU:0, one launch (start us, length us, event | category | flops | bytes accessed | tf_op | source)
XLA Modules:
  0.0 47.1 jit_solution(14848601357008594122)
XLA Ops:
  1.9 43.5 %fused.1 = (bf16[6,6144]{1,0:T(8,128)(2,1)}, f32[48,128]{1,0:T(8,128)}) custom-call(s32[1]{0:T(128)S(6)} %copy.17.lengths_hbm, s32[6]{0:T(128)} %parents_hbm.1, s32[2,6]{1,0:T(2,128)} %bitcast.5, s32[1]{0:T(128)S(6)} %copy.18.accepted_hbm, bf16[6,6144]{1,0:T(8,128)(2,1)} %queries_hbm.1, bf16[6,2,1024]{2,1,0:T(2,128)(2,1)} %tree_hbm.1, ...), custom_call_target="tpu_custom_call" | custom-call | tf_op jit(solution)/shard_map/fused/pallas_call | solution.py:1236
  45.5 1.6 %finish.1 = (bf16[6,6144]{1,0:T(8,128)(2,1)}, bf16[1,6144]{1,0:T(2,128)(2,1)}) custom-call(bf16[6,6144]{1,0:T(8,128)(2,1)} %get-tuple-element.4.layer, f32[48,128]{1,0:T(8,128)} %get-tuple-element.5.draft_lines), custom_call_target="tpu_custom_call" | custom-call | tf_op jit(solution)/shard_map/finish/pallas_call | solution.py:1330

commit v5 on v4

--- a/solution.py
+++ b/solution.py
@@ -473,14 +473,14 @@
 UNIT = 256
 
 
-def greet_all(n, me):
+def greet_near(group, mine, lane):
     barrier = pltpu.get_barrier_semaphore()
-
-    def hello(k, carry):
-        pl.semaphore_signal(barrier, inc=1, device_id={"expert": lax.rem(me + k, n)})
-        return carry
-
-    lax.fori_loop(1, n, hello, 0)
+    for step in range(1, EXPERTS):
+        peer = lax.rem(mine + step, EXPERTS) * group + lane
+        pl.semaphore_signal(barrier, inc=1, device_id={"expert": peer})
+    for step in range(1, group):
+        peer = mine * group + lax.rem(lane + step, group)
+        pl.semaphore_signal(barrier, inc=1, device_id={"expert": peer})
     return barrier
 
 
@@ -532,6 +532,8 @@
     chip_sum,
     chip_leaving,
     chip_returned,
+    direct_leaving,
+    direct_returned,
     home_leaving,
     home_returned,
     pick_rows,
@@ -557,6 +559,8 @@
     core_in_sem,
     chip_out_sem,
     chip_in_sem,
+    direct_out_sem,
+    direct_in_sem,
     home_out_sem,
     home_in_sem,
     pick_out_sem,
@@ -665,7 +669,7 @@
     ]
     for copy in inputs[8:] + inputs[:8]:
         copy.start()
-    barrier = greet_all(n, me)
+    barrier = greet_near(group, mine, lane)
     for copy in inputs[8:]:
         copy.wait()
 
@@ -801,7 +805,7 @@
         arrived[mine, :, cols] = packed[mine, :, cols]
 
     pack_step(0)
-    pl.semaphore_wait(barrier, n - 1)
+    pl.semaphore_wait(barrier, EXPERTS + group - 2)
     for c in range(len(chunks)):
         if c > 0:
             pack_step(c)
@@ -828,10 +832,6 @@
         @pl.when(me == j)
         def _():
             blocks[j] = row[:, b * depth : (b + 1) * depth]
-
-    for b in range(block_count):
-        send_block(embed_row, b, block_count + b)
-        send_block(hidden_row, b, b)
 
     logits = [jnp.zeros((padded, 1), f32) for _ in range(EXPERTS)]
     for k in range(slice_count):
@@ -886,8 +886,13 @@
         pick_rows[e] = jnp.sum(
             jnp.where(token_row == accepted[0], chosen, 0.0), axis=0, keepdims=True
         )
-    for step in range(1, EXPERTS):
-        pick_push(step).start()
+    def send_early():
+        for step in range(1, EXPERTS):
+            pick_push(step).start()
+        for b in range(block_count):
+            send_block(embed_row, b, block_count + b)
+            send_block(hidden_row, b, b)
+
     pick_arrived[mine] = pick_rows[mine]
 
     def row_push(c, which, sem, peer):
@@ -942,6 +947,8 @@
     for t in range(len(chunks) + 3):
         if t < len(chunks):
             gather_step(t)
+        if t == 2:
+            send_early()
         if 0 <= t - 2 < len(chunks):
             forward_step(t - 2)
         if 0 <= t - 3 < len(chunks):
@@ -992,6 +999,22 @@
             )
             partial = value if partial is None else partial + value
             start_load(place[item] + slots)
+        if p == piece_count - 1:
+            for member in range(group):
+                direct_leaving[member] = partial[member * share : (member + 1) * share].astype(
+                    bf16
+                )
+            for step in range(1, group):
+                peer = lax.rem(lane + step, group)
+                push(
+                    direct_leaving.at[peer],
+                    direct_returned.at[lane],
+                    direct_out_sem,
+                    direct_in_sem,
+                    mine * group + peer,
+                ).start()
+            direct_returned[lane] = direct_leaving[lane]
+            return
         for member in range(group):
             block = partial[member * share : (member + 1) * share].astype(bf16)
             a, c = member // 2, member % 2
@@ -1030,10 +1053,16 @@
         )
 
     def chip_step(p, pick_mixers):
-        chip_push(p).wait_recv()
         start, size = pieces[p]
         cols = slice(start, start + size)
-        total = chip_sum[:, cols] + chip_returned[:, cols].astype(f32)
+        if p < piece_count - 1:
+            chip_push(p).wait_recv()
+            total = chip_sum[:, cols] + chip_returned[:, cols].astype(f32)
+        else:
+            awaited(direct_returned.at[0 : group - 1], direct_in_sem).wait_recv()
+            total = direct_returned[0].astype(f32)
+            for member in range(1, group):
+                total = total + direct_returned[member].astype(f32)
         mixed = jnp.dot(pick_mixers, total.astype(bf16), preferred_element_type=f32)
         portion = mixed[:padded] + mixed[padded : 2 * padded] + mixed[2 * padded :]
         for unit in range(start // UNIT, (start + size) // UNIT):
@@ -1149,15 +1178,15 @@
     )
     pick_mixers = split(picks)
 
-    for p in range(piece_count + 3):
-        if p < piece_count:
-            partial_step(p)
-        if 0 <= p - 1 < piece_count:
+    for p in range(piece_count):
+        partial_step(p)
+        if p > 0:
             core_step(p - 1)
-        if p == piece_count:
-            block_step()
-        if 0 <= p - 3 < piece_count:
-            chip_step(p - 3, pick_mixers)
+        if p > 3:
+            chip_step(p - 4, pick_mixers)
+    block_step()
+    for p in range(piece_count - 4, piece_count):
+        chip_step(p, pick_mixers)
     draft_step(0, unit_count - 1, False)
     draft_step(unit_count - 1, unit_count, True)
     awaited(home_returned.at[0 : EXPERTS - 1], home_in_sem).wait_recv()
@@ -1167,8 +1196,10 @@
     awaited(packed.at[0 : EXPERTS - 1], out_sem).wait_send()
     awaited(rows.at[0 : 3 * share, :], plane_out_sem).wait_send()
     awaited(pick_rows.at[0 : EXPERTS - 1], pick_out_sem).wait_send()
-    awaited(leaving, core_out_sem).wait_send()
-    awaited(chip_leaving, chip_out_sem).wait_send()
+    paired = model_width - UNIT
+    awaited(leaving.at[:, :, 0:paired], core_out_sem).wait_send()
+    awaited(chip_leaving.at[:, 0:paired], chip_out_sem).wait_send()
+    awaited(direct_leaving.at[0 : group - 1], direct_out_sem).wait_send()
     awaited(home_leaving.at[0 : EXPERTS - 1], home_out_sem).wait_send()
     awaited(blocks.at[0 : n - 1], block_out_sem).wait_send()
     unit_total = share_leaving.shape[0]
@@ -1229,17 +1260,18 @@
     line_count = model_width // LANES
     kv_width = tree_key_value.shape[2]
     key_rows = key_value_cache.shape[2] + LANES
-    anywhere = pl.BlockSpec(memory_space=pl.ANY)
+    in_hbm = pl.BlockSpec(memory_space=pltpu.HBM)
     whole = pl.BlockSpec(memory_space=pltpu.VMEM)
     bf16, f32 = jnp.bfloat16, jnp.float32
     dma = pltpu.SemaphoreType.DMA
+    pinned = pltpu.with_memory_space_constraint
     layer, draft_lines = pl.pallas_call(
         functools.partial(fused_kernel, n, slots),
         out_shape=(
-            jax.ShapeDtypeStruct((TREE_NODES, model_width), bf16),
-            jax.ShapeDtypeStruct((line_count, LANES), f32),
+            pltpu.VMEM((TREE_NODES, model_width), bf16),
+            pltpu.VMEM((line_count, LANES), f32),
         ),
-        in_specs=[anywhere] * 15,
+        in_specs=[in_hbm] * 15,
         out_specs=(whole, whole),
         scratch_shapes=[
             pltpu.SMEM(lengths.shape, jnp.int32),
@@ -1270,6 +1302,8 @@
             pltpu.VMEM((share, model_width), f32),
             pltpu.VMEM((share, model_width), bf16),
             pltpu.VMEM((share, model_width), bf16),
+            pltpu.VMEM((group, share, UNIT), bf16),
+            pltpu.VMEM((group, share, UNIT), bf16),
             pltpu.VMEM((EXPERTS, CAP, model_width), bf16),
             pltpu.VMEM((EXPERTS, CAP, model_width), bf16),
             pltpu.VMEM((EXPERTS, 1, LANES), f32),
@@ -1295,6 +1329,8 @@
             dma((pieces,)),
             dma,
             dma((pieces,)),
+            dma,
+            dma,
             dma,
             dma,
             dma,
@@ -1336,7 +1372,7 @@
         in_specs=[whole, whole],
         out_specs=(whole, whole),
         name="finish",
-    )(layer, draft_lines)
+    )(pinned(layer, pltpu.VMEM), pinned(draft_lines, pltpu.VMEM))
 
 
 def fits(lengths, gate_weight, draft_fc, n):

time: 47.2 us -> 45 us (0.953)
  Pallas kernels: 45.1 us -> 42.9 us
    pallas_call x1, Pallas kernels: 43.5 us -> 42.2 us  [fused(): pl.pallas_call(functools.partial(fused_kernel, n, slots), out_shape=(pltp...]
    pallas_call x1, Pallas kernels: 1.57 us -> 0.68 us  [fused(): pl.pallas_call(finish_kernel, out_shape=(jax.ShapeDtypeStruct((TREE_NODES...]
where the time goes in v5:
time: 45 us; the launch traced here: 44.8 us
  Pallas kernels  42.9 us (95%)
  between operations  1.93 us (4%)
    pallas_call x1, Pallas kernels, fused(): pl.pallas_call(functools.partial(fused_kernel, n, slots), out_shape=(pltp...  42.2 us

profile of v5, /device:TPU:0, one launch (start us, length us, event | category | flops | bytes accessed | tf_op | source)
XLA Modules:
  0.0 44.8 jit_solution(5750211971762029160)
XLA Ops:
  1.9 42.2 %fused.1 = (bf16[6,6144]{1,0:T(8,128)(2,1)S(1)}, f32[48,128]{1,0:T(8,128)S(1)}) custom-call(s32[1]{0:T(128)S(6)} %copy.17.lengths_hbm, s32[6]{0:T(128)} %parents_hbm.1, s32[2,6]{1,0:T(2,128)} %bitcast.5, s32[1]{0:T(128)S(6)} %copy.18.accepted_hbm, bf16[6,6144]{1,0:T(8,128)(2,1)} %queries_hbm.1, bf16[6,2,1024]{2,1,0:T(2,128)(2,1)} %tree_hbm.1, ...), custom_call_target="tpu_custom_call" | custom-call | tf_op jit(solution)/shard_map/fused/pallas_call | solution.py:1268
  44.2 0.7 %finish.1 = (bf16[6,6144]{1,0:T(8,128)(2,1)}, bf16[1,6144]{1,0:T(2,128)(2,1)}) custom-call(bf16[6,6144]{1,0:T(8,128)(2,1)S(1)} %get-tuple-element.4.layer, f32[48,128]{1,0:T(8,128)S(1)} %get-tuple-element.5.draft_lines), custom_call_target="tpu_custom_call" | custom-call | tf_op jit(solution)/shard_map/finish/pallas_call | solution.py:1366

commit v6 on v5

--- a/solution.py
+++ b/solution.py
@@ -526,20 +526,19 @@
     gate_sum,
     up_sum,
     activation,
-    kept,
     leaving,
     returned,
     chip_sum,
     chip_leaving,
     chip_returned,
-    direct_leaving,
-    direct_returned,
     home_leaving,
     home_returned,
     pick_rows,
     pick_arrived,
     shares,
     share_leaving,
+    late_shares,
+    late_leaving,
     share_rows,
     hidden_row,
     embed_row,
@@ -547,6 +546,8 @@
     block_rows,
     draft_sum,
     draft_wide,
+    pair_leaving,
+    pair_returned,
     draft_leaving,
     draft_returned,
     load_sem,
@@ -559,16 +560,17 @@
     core_in_sem,
     chip_out_sem,
     chip_in_sem,
-    direct_out_sem,
-    direct_in_sem,
     home_out_sem,
     home_in_sem,
     pick_out_sem,
     pick_in_sem,
     share_out_sem,
+    late_out_sem,
     share_in_sem,
     block_out_sem,
     block_in_sem,
+    pair_out_sem,
+    pair_in_sem,
     draft_out_sem,
     draft_in_sem,
 ):
@@ -594,6 +596,8 @@
     piece_count = len(pieces)
     unit_count = depth // UNIT
     block_count = model_width // depth
+    late_block = block_count // 2
+    late_unit = late_block * unit_count
     padded = 8
     share = EXPERTS * CAP
     cache_slots = cache_hbm.shape[2]
@@ -601,6 +605,7 @@
     line_count = model_width // LANES
     lines = SLICE // LANES
     part_count = draft_leaving.shape[0]
+    each = line_count // part_count
 
     pairs = [
         ("pair", k, h, i) for k in range(slice_count) for h in range(half_count) for i in range(2)
@@ -688,7 +693,7 @@
     slot_ids = lax.broadcasted_iota(jnp.int32, (padded, cache_slots), 1)
     bias = jnp.concatenate(
         [
-            jnp.where(slot_ids < lengths[0], 0.0, -1e30),
+            jnp.where(slot_ids < lengths[0, 0], 0.0, -1e30),
             jnp.where(related > 0.5, 0.0, -1e30),
         ],
         axis=1,
@@ -817,7 +822,7 @@
     for k in range(slice_count):
         cols = slice(k * SLICE, (k + 1) * SLICE)
         hidden_row[:, cols] = jnp.sum(
-            jnp.where(token_row == accepted[0], hidden[:, cols], 0.0), axis=0, keepdims=True
+            jnp.where(token_row == accepted[0, 0], hidden[:, cols], 0.0), axis=0, keepdims=True
         )
 
     def block_push(row, b, j):
@@ -865,14 +870,15 @@
 
     mixers = split(weighted)
 
-    def pick_push(step):
+    def pick_push(step, turn):
         plane = lax.rem(mine + step, EXPERTS)
+        column = lax.rem(across + turn, 2)
         return push(
             pick_rows.at[plane],
-            pick_arrived.at[mine],
+            pick_arrived.at[across * EXPERTS + mine],
             pick_out_sem,
             pick_in_sem,
-            plane * group + lane,
+            plane * group + column * 2 + core,
         )
 
     for e in range(EXPERTS):
@@ -884,16 +890,18 @@
             here = (col8 == mine * CAP + position - expert * CAP) & (expert == e)
             chosen = chosen + jnp.where(here, portion, 0.0)
         pick_rows[e] = jnp.sum(
-            jnp.where(token_row == accepted[0], chosen, 0.0), axis=0, keepdims=True
+            jnp.where(token_row == accepted[0, 0], chosen, 0.0), axis=0, keepdims=True
         )
     def send_early():
-        for step in range(1, EXPERTS):
-            pick_push(step).start()
+        for step in range(EXPERTS):
+            for turn in range(2):
+                if step + turn > 0:
+                    pick_push(step, turn).start()
         for b in range(block_count):
             send_block(embed_row, b, block_count + b)
             send_block(hidden_row, b, b)
 
-    pick_arrived[mine] = pick_rows[mine]
+    pick_arrived[across * EXPERTS + mine] = pick_rows[mine]
 
     def row_push(c, which, sem, peer):
         start, size = chunks[c]
@@ -960,7 +968,7 @@
     def core_push(p):
         cols = piece_cols(p)
         return push(
-            leaving.at[:, :, cols],
+            leaving.at[1 - core, :, :, cols],
             returned.at[:, :, cols],
             core_out_sem,
             core_in_sem.at[p],
@@ -999,33 +1007,9 @@
             )
             partial = value if partial is None else partial + value
             start_load(place[item] + slots)
-        if p == piece_count - 1:
-            for member in range(group):
-                direct_leaving[member] = partial[member * share : (member + 1) * share].astype(
-                    bf16
-                )
-            for step in range(1, group):
-                peer = lax.rem(lane + step, group)
-                push(
-                    direct_leaving.at[peer],
-                    direct_returned.at[lane],
-                    direct_out_sem,
-                    direct_in_sem,
-                    mine * group + peer,
-                ).start()
-            direct_returned[lane] = direct_leaving[lane]
-            return
         for member in range(group):
             block = partial[member * share : (member + 1) * share].astype(bf16)
-            a, c = member // 2, member % 2
-
-            @pl.when(core == c)
-            def _():
-                kept[a, :, cols] = block
-
-            @pl.when(core != c)
-            def _():
-                leaving[a, :, cols] = block
+            leaving[member % 2, member // 2, :, cols] = block
 
         core_push(p).start()
 
@@ -1035,55 +1019,72 @@
         cols = slice(start, start + size)
         far = 1 - across
         chip_leaving[:, cols] = (
-            kept[far, :, cols].astype(f32) + returned[far, :, cols].astype(f32)
+            leaving[core, far, :, cols].astype(f32) + returned[far, :, cols].astype(f32)
         ).astype(bf16)
         chip_push(p).start()
-        chip_sum[:, cols] = kept[across, :, cols].astype(f32) + returned[across, :, cols].astype(
+        chip_sum[:, cols] = leaving[core, across, :, cols].astype(f32) + returned[across, :, cols].astype(
             f32
         )
-
-    def share_push(unit, b):
-        part = unit % unit_count
-        return push(
-            share_leaving.at[unit],
-            shares.at[part, me],
-            share_out_sem,
-            share_in_sem.at[part // (unit_count - 1)],
-            b,
-        )
-
-    def chip_step(p, pick_mixers):
+        if start < late_unit * UNIT:
+            return
+        portions = [
+            portion_of(
+                both_mixers[column],
+                leaving[core, column, :, cols].astype(f32) + returned[column, :, cols].astype(f32),
+            )
+            for column in range(2)
+        ]
+        send_shares(start, size, jnp.concatenate(portions, axis=0))
+
+    def portion_of(pick_mixers, total):
+        mixed = jnp.dot(pick_mixers, total.astype(bf16), preferred_element_type=f32)
+        portion = mixed[:padded] + mixed[padded : 2 * padded] + mixed[2 * padded :]
+        return portion[:EXPERTS]
+
+    def send_shares(start, size, portion):
+        for unit in range(start // UNIT, (start + size) // UNIT):
+            b, part = unit // unit_count, unit % unit_count
+            first = unit * UNIT - start
+            value = portion[:, first : first + UNIT].astype(bf16)
+            if unit < late_unit:
+                source, target, sem = share_leaving.at[unit], shares, share_out_sem
+            else:
+                source, target, sem = late_leaving.at[unit - late_unit], late_shares, late_out_sem
+
+            source[...] = value
+
+            @pl.when(me != b)
+            def _():
+                push(
+                    source,
+                    target.at[part, me],
+                    sem,
+                    share_in_sem.at[part // (unit_count - 1)],
+                    b,
+                ).start()
+
+            @pl.when(me == b)
+            def _():
+                target[part, b] = value
+
+    held_back = 3
+
+    def leave_step(p):
+        for step in range(1, EXPERTS):
+            to_home(p, step).start()
+
+    def chip_step(p):
         start, size = pieces[p]
         cols = slice(start, start + size)
-        if p < piece_count - 1:
-            chip_push(p).wait_recv()
-            total = chip_sum[:, cols] + chip_returned[:, cols].astype(f32)
-        else:
-            awaited(direct_returned.at[0 : group - 1], direct_in_sem).wait_recv()
-            total = direct_returned[0].astype(f32)
-            for member in range(1, group):
-                total = total + direct_returned[member].astype(f32)
-        mixed = jnp.dot(pick_mixers, total.astype(bf16), preferred_element_type=f32)
-        portion = mixed[:padded] + mixed[padded : 2 * padded] + mixed[2 * padded :]
-        for unit in range(start // UNIT, (start + size) // UNIT):
-            b = unit // unit_count
-            first = unit * UNIT - start
-            value = portion[:EXPERTS, first : first + UNIT].astype(bf16)
-
-            @pl.when(me != b)
-            def _():
-                share_leaving[unit] = value
-                share_push(unit, b).start()
-
-            @pl.when(me == b)
-            def _():
-                shares[unit % unit_count, b] = value
-
+        chip_push(p).wait_recv()
+        total = chip_sum[:, cols] + chip_returned[:, cols].astype(f32)
+        if start < late_unit * UNIT:
+            send_shares(start, size, portion_of(own_mixers, total))
         for s in range(EXPERTS):
             home_leaving[s, :, cols] = total[s * CAP : (s + 1) * CAP].astype(bf16)
-        for step in range(1, EXPERTS):
-            to_home(p, step).start()
         home_returned[mine, :, cols] = home_leaving[mine, :, cols]
+        if p >= held_back:
+            leave_step(p)
 
     def home_step(p):
         start, size = pieces[p]
@@ -1096,17 +1097,27 @@
         result = (hidden[:, cols] + expert_sum).astype(bf16)
         layer_out[:, cols] = result[:TREE_NODES]
 
-    def draft_push(q, peer, at):
+    pair_rows_count = n // 2
+    own_place = across * EXPERTS + mine
+
+    def pair_push(q):
         return push(
-            draft_leaving.at[q, peer],
-            draft_returned.at[q, at],
+            pair_leaving.at[q], pair_returned.at[q], pair_out_sem, pair_in_sem.at[q], core_peer
+        )
+
+    def draft_push(q, row):
+        peer = lax.rem(row, EXPERTS) * group + row // EXPERTS * 2 + core
+        return push(
+            draft_leaving.at[q, row],
+            draft_returned.at[q, me // 2],
             draft_out_sem,
             draft_in_sem,
             peer,
         )
 
     def row_of(device):
-        return lax.rem(device, group) * EXPERTS + device // group
+        column = lax.rem(device, group) // 2
+        return lax.rem(device, 2) * pair_rows_count + column * EXPERTS + device // group
 
     def block_step():
         awaited(blocks.at[0 : n - 1], block_in_sem).wait_recv()
@@ -1119,13 +1130,31 @@
         share_rows[...] = jnp.zeros_like(share_rows)
 
     def share_step(first, past):
-        @pl.when(me < block_count)
+        sem = share_in_sem.at[first // (unit_count - 1)]
+
+        @pl.when((me >= late_block) & (me < block_count))
         def _():
-            sem = share_in_sem.at[first // (unit_count - 1)]
+            awaited(late_shares.at[first:past, 0 : n - 1], sem).wait_recv()
+            for part in range(first, past):
+                totals = []
+                for c in range(2):
+                    total = late_shares[part, c].astype(f32)
+                    for member in range(c + 2, n, 2):
+                        total = total + late_shares[part, member].astype(f32)
+                    totals.append(total)
+                sums = [
+                    totals[c][column * EXPERTS : (column + 1) * EXPERTS]
+                    for c in range(2)
+                    for column in range(2)
+                ]
+                share_rows[:, part * UNIT : (part + 1) * UNIT] = jnp.concatenate(sums, axis=0)
+
+        @pl.when(me < late_block)
+        def _():
             awaited(shares.at[first:past, 0 : n - 1], sem).wait_recv()
             for part in range(first, past):
                 sums = []
-                for member in range(group):
+                for member in (0, 2, 1, 3):
                     total = shares[part, member].astype(f32)
                     for e in range(1, EXPERTS):
                         total = total + shares[part, e * group + member].astype(f32)
@@ -1157,67 +1186,88 @@
                     ]
             if not final:
                 continue
-            each = line_count // part_count
-            for row in range(n):
-                device = row % EXPERTS * group + row // EXPERTS
-                start = row * line_count + q * each
-                draft_leaving[q, device] = draft_wide[start : start + each, :].astype(bf16)
-
-            def send_partial(k, carry):
-                draft_push(q, lax.rem(me + k, n), me).start()
-                return carry
-
-            lax.fori_loop(1, n, send_partial, 0)
-            draft_returned[q, me] = draft_leaving[q, me]
-
-    awaited(pick_arrived.at[0 : EXPERTS - 1], pick_in_sem).wait_recv()
-    picks = jnp.concatenate(
-        [pick_arrived[s][:, :share] for s in range(EXPERTS)]
-        + [jnp.zeros((padded - EXPERTS, share), f32)],
-        axis=0,
-    )
-    pick_mixers = split(picks)
+            for i in range(pair_rows_count):
+                start = ((1 - core) * pair_rows_count + i) * line_count + q * each
+                pair_leaving[q, i] = draft_wide[
+                    pl.ds(pl.multiple_of(start, each), each), :
+                ].astype(bf16)
+            pair_push(q).start()
+
+    def pair_step(q):
+        pair_push(q).wait_recv()
+        for i in range(pair_rows_count):
+            start = (core * pair_rows_count + i) * line_count + q * each
+            total = draft_wide[pl.ds(pl.multiple_of(start, each), each), :] + pair_returned[
+                q, i
+            ].astype(f32)
+            draft_leaving[q, i] = total.astype(bf16)
+
+        def send_partial(k, carry):
+            draft_push(q, lax.rem(own_place + k, pair_rows_count)).start()
+            return carry
+
+        lax.fori_loop(1, pair_rows_count, send_partial, 0)
+        draft_returned[q, me // 2] = draft_leaving[q, own_place]
+
+    pick_total = pick_arrived.shape[0]
+    awaited(pick_arrived.at[0 : pick_total - 1], pick_in_sem).wait_recv()
+
+    def mixers_of(column):
+        picks = [pick_arrived[column * EXPERTS + s][:, :share] for s in range(EXPERTS)]
+        picks.append(jnp.zeros((padded - EXPERTS, share), f32))
+        return split(jnp.concatenate(picks, axis=0))
+
+    own_mixers = mixers_of(across)
+    both_mixers = [mixers_of(column) for column in range(2)]
 
     for p in range(piece_count):
         partial_step(p)
         if p > 0:
             core_step(p - 1)
-        if p > 3:
-            chip_step(p - 4, pick_mixers)
+        if p >= 4:
+            chip_step(p - 4)
+    core_step(piece_count - 1)
+    for p in range(held_back):
+        leave_step(p)
     block_step()
     for p in range(piece_count - 4, piece_count):
-        chip_step(p, pick_mixers)
+        chip_step(p)
     draft_step(0, unit_count - 1, False)
     draft_step(unit_count - 1, unit_count, True)
+    for q in range(part_count):
+        pair_step(q)
     awaited(home_returned.at[0 : EXPERTS - 1], home_in_sem).wait_recv()
     for p in range(piece_count):
         home_step(p)
 
     awaited(packed.at[0 : EXPERTS - 1], out_sem).wait_send()
     awaited(rows.at[0 : 3 * share, :], plane_out_sem).wait_send()
-    awaited(pick_rows.at[0 : EXPERTS - 1], pick_out_sem).wait_send()
-    paired = model_width - UNIT
-    awaited(leaving.at[:, :, 0:paired], core_out_sem).wait_send()
-    awaited(chip_leaving.at[:, 0:paired], chip_out_sem).wait_send()
-    awaited(direct_leaving.at[0 : group - 1], direct_out_sem).wait_send()
+    awaited(pick_arrived.at[0 : pick_total - 1], pick_out_sem).wait_send()
+    awaited(leaving.at[0], core_out_sem).wait_send()
+    awaited(chip_leaving, chip_out_sem).wait_send()
     awaited(home_leaving.at[0 : EXPERTS - 1], home_out_sem).wait_send()
     awaited(blocks.at[0 : n - 1], block_out_sem).wait_send()
-    unit_total = share_leaving.shape[0]
-
-    @pl.when(me < block_count)
-    def _():
-        awaited(share_leaving.at[0 : unit_total - unit_count], share_out_sem).wait_send()
-
-    @pl.when(me >= block_count)
-    def _():
-        awaited(share_leaving, share_out_sem).wait_send()
-
-    awaited(draft_leaving.at[:, 0 : n - 1], draft_out_sem).wait_send()
-    awaited(draft_returned.at[:, 0 : n - 1], draft_in_sem).wait_recv()
-    each = line_count // part_count
+    for low, past, buffer, sem in (
+        (0, late_block, share_leaving, share_out_sem),
+        (late_block, block_count, late_leaving, late_out_sem),
+    ):
+        total = buffer.shape[0]
+        owner = (me >= low) & (me < past)
+
+        @pl.when(owner)
+        def _():
+            awaited(buffer.at[0 : total - unit_count], sem).wait_send()
+
+        @pl.when(jnp.logical_not(owner))
+        def _():
+            awaited(buffer, sem).wait_send()
+
+    awaited(pair_leaving, pair_out_sem).wait_send()
+    awaited(draft_leaving.at[:, 0 : pair_rows_count - 1], draft_out_sem).wait_send()
+    awaited(draft_returned.at[:, 0 : pair_rows_count - 1], draft_in_sem).wait_recv()
     for q in range(part_count):
         total = draft_returned[q, 0].astype(f32)
-        for source in range(1, n):
+        for source in range(1, pair_rows_count):
             total = total + draft_returned[q, source].astype(f32)
         draft_out[q * each : (q + 1) * each, :] = total
 
@@ -1274,10 +1324,10 @@
         in_specs=[in_hbm] * 15,
         out_specs=(whole, whole),
         scratch_shapes=[
-            pltpu.SMEM(lengths.shape, jnp.int32),
+            pltpu.SMEM((1, 1), jnp.int32),
             pltpu.SMEM(parents.shape, jnp.int32),
             pltpu.SMEM(routes.T.shape, jnp.int32),
-            pltpu.SMEM(accepted.shape, jnp.int32),
+            pltpu.SMEM((1, 1), jnp.int32),
             pltpu.VMEM((slots, SLICE, SLICE), bf16),
             pltpu.VMEM((TREE_NODES, model_width), bf16),
             pltpu.VMEM((TREE_NODES, 2, kv_width), bf16),
@@ -1296,20 +1346,19 @@
             pltpu.VMEM((group * share, width), f32),
             pltpu.VMEM((group * share, width), f32),
             pltpu.VMEM((halves, group * share, SLICE), bf16),
-            pltpu.VMEM((2, share, model_width), bf16),
-            pltpu.VMEM((2, share, model_width), bf16),
+            pltpu.VMEM((2, 2, share, model_width), bf16),
             pltpu.VMEM((2, share, model_width), bf16),
             pltpu.VMEM((share, model_width), f32),
             pltpu.VMEM((share, model_width), bf16),
             pltpu.VMEM((share, model_width), bf16),
-            pltpu.VMEM((group, share, UNIT), bf16),
-            pltpu.VMEM((group, share, UNIT), bf16),
             pltpu.VMEM((EXPERTS, CAP, model_width), bf16),
             pltpu.VMEM((EXPERTS, CAP, model_width), bf16),
             pltpu.VMEM((EXPERTS, 1, LANES), f32),
-            pltpu.VMEM((EXPERTS, 1, LANES), f32),
+            pltpu.VMEM((2 * EXPERTS, 1, LANES), f32),
             pltpu.VMEM((units, n, EXPERTS, UNIT), bf16),
-            pltpu.VMEM((model_width // UNIT, EXPERTS, UNIT), bf16),
+            pltpu.VMEM((model_width // UNIT // 2, EXPERTS, UNIT), bf16),
+            pltpu.VMEM((units, n, 2 * EXPERTS, UNIT), bf16),
+            pltpu.VMEM((model_width // UNIT // 2, 2 * EXPERTS, UNIT), bf16),
             pltpu.VMEM((n, depth), f32),
             pltpu.VMEM((1, model_width), f32),
             pltpu.VMEM((1, model_width), f32),
@@ -1317,8 +1366,10 @@
             pltpu.VMEM((n, depth), f32),
             pltpu.VMEM((n, model_width), f32),
             pltpu.VMEM((n * line_count, LANES), f32),
-            pltpu.VMEM((parts, n, line_count // parts, LANES), bf16),
-            pltpu.VMEM((parts, n, line_count // parts, LANES), bf16),
+            pltpu.VMEM((parts, n // 2, line_count // parts, LANES), bf16),
+            pltpu.VMEM((parts, n // 2, line_count // parts, LANES), bf16),
+            pltpu.VMEM((parts, n // 2, line_count // parts, LANES), bf16),
+            pltpu.VMEM((parts, n // 2, line_count // parts, LANES), bf16),
             dma((10,)),
             dma((12,)),
             dma,
@@ -1335,10 +1386,11 @@
             dma,
             dma,
             dma,
-            dma,
             dma((2,)),
             dma,
             dma,
+            dma,
+            dma((parts,)),
             dma,
             dma,
         ],
@@ -1347,10 +1399,10 @@
         ),
         name="fused",
     )(
-        lengths,
+        lengths.reshape(1, 1),
         parents,
         routes.T,
-        accepted,
+        accepted.reshape(1, 1),
         queries,
         tree_key_value,
         key_value_cache,
@@ -1387,6 +1439,8 @@
         and depth > UNIT
         and depth <= SLICE
         and n * depth == 2 * model_width
+        and model_width // depth * depth == model_width
+        and model_width // depth // 2 * depth == 3 * SLICE
     )
 
 

time: 45 us -> 43.7 us (0.971)
  Pallas kernels: 42.9 us -> 41.6 us
    pallas_call x1, Pallas kernels: 42.2 us -> 40.9 us  [fused(): pl.pallas_call(functools.partial(fused_kernel, n, slots), out_shape=(pltp...]
where the time goes in v6:
time: 43.7 us; the launch traced here: 43.5 us
  Pallas kernels  41.6 us (95%)
  between operations  1.93 us (4%)
    pallas_call x1, Pallas kernels, fused(): pl.pallas_call(functools.partial(fused_kernel, n, slots), out_shape=(pltp...  40.9 us

profile of v6, /device:TPU:0, one launch (start us, length us, event | category | flops | bytes accessed | tf_op | source)
XLA Modules:
  0.0 43.5 jit_solution(8274092689480181649)
XLA Ops:
  1.9 40.9 %fused.1 = (bf16[6,6144]{1,0:T(8,128)(2,1)S(1)}, f32[48,128]{1,0:T(8,128)S(1)}) custom-call(s32[1,1]{1,0:T(1,128)} %bitcast.5.lengths_hbm, s32[6]{0:T(128)} %parents_hbm.1, s32[2,6]{1,0:T(2,128)} %bitcast.9, s32[1,1]{1,0:T(1,128)} %bitcast.6.accepted_hbm, bf16[6,6144]{1,0:T(8,128)(2,1)} %queries_hbm.1, bf16[6,2,1024]{2,1,0:T(2,128)(2,1)} %tree_hbm.1, ...), custom_call_target="tpu_custom_call" | custom-call | tf_op jit(solution)/shard_map/fused/pallas_call | solution.py:1318
  42.8 0.7 %finish.1 = (bf16[6,6144]{1,0:T(8,128)(2,1)}, bf16[1,6144]{1,0:T(2,128)(2,1)}) custom-call(bf16[6,6144]{1,0:T(8,128)(2,1)S(1)} %get-tuple-element.4.layer, f32[48,128]{1,0:T(8,128)S(1)} %get-tuple-element.5.draft_lines), custom_call_target="tpu_custom_call" | custom-call | tf_op jit(solution)/shard_map/finish/pallas_call | solution.py:1418

commit v7 on v6

--- a/solution.py
+++ b/solution.py
@@ -589,7 +589,7 @@
     slice_count = model_width // SLICE
     half_count = width // SLICE
     half = SLICE // 2
-    chunks = [(0, half), (half, half)] + [(k * SLICE, SLICE) for k in range(1, slice_count)]
+    chunks = [(0, UNIT), (UNIT, SLICE - UNIT)] + [(k * SLICE, SLICE) for k in range(1, slice_count)]
     last = model_width - SLICE
     pieces = [(k * SLICE, SLICE) for k in range(slice_count - 1)]
     pieces += [(last, SLICE - UNIT), (model_width - UNIT, UNIT)]

time: 43.7 us -> 43.5 us (level)
  no operation moved by 1% of the time
where the time goes in v7:
time: 43.5 us; the launch traced here: 43.4 us
  Pallas kernels  41.4 us (95%)
  between operations  1.93 us (4%)
    pallas_call x1, Pallas kernels, fused(): pl.pallas_call(functools.partial(fused_kernel, n, slots), out_shape=(pltp...  40.8 us

profile of v7, /device:TPU:0, one launch (start us, length us, event | category | flops | bytes accessed | tf_op | source)
XLA Modules:
  0.0 43.4 jit_solution(16449264459317788174)
XLA Ops:
  1.9 40.8 %fused.1 = (bf16[6,6144]{1,0:T(8,128)(2,1)S(1)}, f32[48,128]{1,0:T(8,128)S(1)}) custom-call(s32[1,1]{1,0:T(1,128)} %bitcast.5.lengths_hbm, s32[6]{0:T(128)} %parents_hbm.1, s32[2,6]{1,0:T(2,128)} %bitcast.9, s32[1,1]{1,0:T(1,128)} %bitcast.6.accepted_hbm, bf16[6,6144]{1,0:T(8,128)(2,1)} %queries_hbm.1, bf16[6,2,1024]{2,1,0:T(2,128)(2,1)} %tree_hbm.1, ...), custom_call_target="tpu_custom_call" | custom-call | tf_op jit(solution)/shard_map/fused/pallas_call | solution.py:1318
  42.7 0.7 %finish.1 = (bf16[6,6144]{1,0:T(8,128)(2,1)}, bf16[1,6144]{1,0:T(2,128)(2,1)}) custom-call(bf16[6,6144]{1,0:T(8,128)(2,1)S(1)} %get-tuple-element.4.layer, f32[48,128]{1,0:T(8,128)S(1)} %get-tuple-element.5.draft_lines), custom_call_target="tpu_custom_call" | custom-call | tf_op jit(solution)/shard_map/finish/pallas_call | solution.py:1418
